TPU v7x, 512 devices: a whole 4x8x8 slice. The times are simulated.
512 devices in a mesh: segment: 4 (over x), shard: 128 (over z, y, core).
Axes of the slice: x: 4, y: 8, z: 8, core: 2. Of those that a mesh axis runs over, the one named last changes fastest.
Arguments:
- proposal_attributes: bfloat16 [2, 65536, 1024], P(None, 'shard'), may hold values from -6 to 6
- keeper_ordering_vectors: bfloat16 [2, 16384, 4096], P(None, 'shard'), may hold values from -6 to 6
- keeper_positions: int32 [2, 16384], P(None, 'shard'), may hold values from 0 to 511
- alive_tallies: int32 [2, 128], P(None, 'shard'), may hold values from 256 to 512
- holder_shards: int32 [2, 16384, 1], P(None, 'shard'), may hold values from 0 to 127; in each aligned block of 128 rows (0 to 127, 128 to 255, ..., all dimensions but the last counted through in order) at most 2 rows name the same one
- holder_attribute_factor: bfloat16 [128, 4096], P('shard'), may hold values from 0.099609375 to 1.8984375
- early_inner_matrix: bfloat16 [1024, 1024], replicated, may hold values from -0.1875 to 0.1875
- early_inner_offset: float32 [1024], replicated, may hold values from -3 to 3
- early_grading_vector: bfloat16 [1024], replicated, may hold values from -0.1875 to 0.1875
- block_lowering_matrices: bfloat16 [3, 4096, 128], P(None, 'shard'), may hold values from -0.09375 to 0.09375
- block_raising_flipped: bfloat16 [3, 4096, 128], P(None, 'shard'), may hold values from -0.5 to 0.5
- block_result_offsets: float32 [3, 4096], replicated, may hold values from -3 to 3
- block_grading_vectors: float32 [3, 4096], replicated, may hold values from -0.09375 to 0.09375
Outputs:
- exits: float32 [4, 2, 32768], P('segment', None, 'shard')
Inputs may be any that keep to these rules, and one draw needn't show every extreme that they name: `holder_shards`: in every round at most 2 entries of one block of 128 go to one owner. `keeper_positions`: entries at or above the block's count in alive_tallies are padding.
All inputs are finite; a program needn't handle non-finite values.
Results may differ from a plain program's by a relative error of at most 0.02.
Values may be sent and summed in bfloat16 or wider, within the bound.
A program may use at most 64 MiB of HBM per device.

v0:
```python
import jax
import jax.numpy as jnp
from jax import lax
from jax.sharding import PartitionSpec as P


def shifted(value, axis, by):
    size = lax.axis_size(axis)
    pairs = [(i, i + by) for i in range(size) if 0 <= i + by < size]
    return lax.ppermute(value, axis, pairs)


def slot_matrix(owner_col, shard_count, cap_slots):
    columns = jnp.arange(shard_count, dtype=jnp.int32)
    onehot = (owner_col[:, None] == columns[None, :]).astype(jnp.int32)
    before = jnp.cumsum(onehot, axis=0) - onehot
    slot_within = jnp.sum(before * onehot, axis=1)
    target = owner_col * cap_slots + slot_within
    positions = jnp.arange(shard_count * cap_slots, dtype=jnp.int32)
    return (positions[:, None] == target[None, :]).astype(jnp.float32)


def prerank_rows(
    cand_block,
    chosen_elements,
    cand_count,
    row_block,
    early_inner_matrix,
    early_inner_offset,
    early_grading_vector,
):
    hidden = jax.nn.relu(
        jnp.dot(cand_block, early_inner_matrix, preferred_element_type=jnp.float32)
        + early_inner_offset
    ).astype(jnp.bfloat16)
    scores = jnp.dot(hidden, early_grading_vector, preferred_element_type=jnp.float32)
    keep_mask = (chosen_elements < cand_count).astype(jnp.float32)
    sigmoid_factors = jax.nn.sigmoid(scores[chosen_elements]) * keep_mask
    modulated_vectors = (row_block.astype(jnp.float32) * sigmoid_factors[:, None]).astype(
        jnp.bfloat16
    )
    return (modulated_vectors, sigmoid_factors)


def rank_section(
    row_block, flag_vals, gain_rows, up_weight, back_weight, bias_vec, head_vec, crossing
):
    scaled = (row_block.astype(jnp.float32) * gain_rows).astype(jnp.bfloat16)
    row_block = jnp.where(crossing, scaled, row_block)
    inner_proj = jnp.dot(row_block, up_weight, preferred_element_type=jnp.float32)
    active = jnp.where(crossing, inner_proj, jax.nn.relu(inner_proj)).astype(jnp.bfloat16)
    lifted = (
        lax.dot_general(
            active, back_weight, (((1,), (1,)), ((), ())), preferred_element_type=jnp.float32
        )
        + bias_vec
    )
    base_rows = row_block.astype(jnp.float32)
    result = (base_rows + jnp.where(crossing, base_rows * lifted, lifted)) * flag_vals[:, None]
    raw_activations = jnp.sum(result * head_vec, axis=1)
    return (result.astype(jnp.bfloat16), raw_activations)


def local(
    proposal_attributes,
    keeper_ordering_vectors,
    keeper_positions,
    alive_tallies,
    holder_shards,
    holder_attribute_factor,
    early_inner_matrix,
    early_inner_offset,
    early_grading_vector,
    block_lowering_matrices,
    block_raising_flipped,
    block_result_offsets,
    block_grading_vectors,
):
    segment_id = lax.axis_index("segment")
    segment_count = lax.axis_size("segment")
    shard_count = lax.axis_size("shard")
    round_total = proposal_attributes.shape[0]
    retained_tally = keeper_ordering_vectors.shape[1]
    vector_length = keeper_ordering_vectors.shape[2]
    cap_slots = max(2, 2 * retained_tally // shard_count)
    slot_count = shard_count * cap_slots
    section_pick = jnp.clip(segment_id - 1, 0, 2)
    up_local = lax.dynamic_slice_in_dim(block_lowering_matrices, section_pick, 1, 0)
    back_local = lax.dynamic_slice_in_dim(block_raising_flipped, section_pick, 1, 0)
    up_all, back_all = (
        lax.all_gather(up_local, "shard", axis=1, tiled=True),
        lax.all_gather(back_local, "shard", axis=1, tiled=True),
    )
    up_weight = up_all[0]
    back_weight = back_all[0]
    bias_vec = lax.dynamic_index_in_dim(block_result_offsets, section_pick, 0, keepdims=False)
    head_vec = lax.dynamic_index_in_dim(block_grading_vectors, section_pick, 0, keepdims=False)
    crossing = segment_id == 1
    is_first = segment_id == 0
    results = jnp.zeros((round_total, slot_count), jnp.float32)
    carried = jnp.zeros((slot_count, vector_length), jnp.bfloat16)
    carried_flags = jnp.zeros((slot_count,), jnp.bfloat16)
    own_gain = holder_attribute_factor[0].astype(jnp.float32)
    for tick_index in range(round_total + segment_count - 1):
        work_round = tick_index - segment_id
        is_live = (work_round >= 0) & (work_round < round_total)
        query_pass_portion = jnp.clip(work_round, 0, round_total - 1)
        chosen_elements = lax.dynamic_index_in_dim(
            keeper_positions, query_pass_portion, 0, keepdims=False
        )
        cand_count = lax.dynamic_index_in_dim(alive_tallies, query_pass_portion, 0, keepdims=False)
        owner_col = lax.dynamic_index_in_dim(holder_shards, query_pass_portion, 0, keepdims=False)[
            :, 0
        ]
        placement = slot_matrix(owner_col, shard_count, cap_slots)
        keep_mask = (chosen_elements < cand_count).astype(jnp.float32)

        def pre_segment():
            cand_block = lax.dynamic_index_in_dim(
                proposal_attributes, query_pass_portion, 0, keepdims=False
            )
            row_block = lax.dynamic_index_in_dim(
                keeper_ordering_vectors, query_pass_portion, 0, keepdims=False
            )
            return prerank_rows(
                cand_block,
                chosen_elements,
                cand_count,
                row_block,
                early_inner_matrix,
                early_inner_offset,
                early_grading_vector,
            )

        def first_segment():
            modulated_vectors, sigmoid_factors = pre_segment()
            sent_rows = jnp.dot(
                placement.astype(jnp.bfloat16),
                modulated_vectors,
                preferred_element_type=jnp.float32,
            ).astype(jnp.bfloat16)
            flag_vals = jnp.sum(placement * keep_mask[None, :], axis=1).astype(jnp.bfloat16)
            values = jnp.sum(placement * sigmoid_factors[None, :], axis=1)
            return (sent_rows, flag_vals, values)

        def later_segment():
            out_rows, raw_activations = rank_section(
                carried,
                carried_flags.astype(jnp.float32),
                own_gain,
                up_weight,
                back_weight,
                bias_vec,
                head_vec,
                crossing,
            )
            return (out_rows, carried_flags, raw_activations)

        if tick_index < round_total:
            out_rows, out_flags, values = lax.cond(is_first, first_segment, later_segment)
            moved_rows, moved_flags = (
                lax.all_to_all(
                    out_rows.reshape(shard_count, cap_slots, vector_length),
                    "shard",
                    split_axis=0,
                    concat_axis=0,
                    tiled=True,
                ),
                lax.all_to_all(
                    out_flags.reshape(shard_count, cap_slots),
                    "shard",
                    split_axis=0,
                    concat_axis=0,
                    tiled=True,
                ),
            )
            out_rows = jnp.where(is_first, moved_rows.reshape(slot_count, vector_length), out_rows)
            out_flags = jnp.where(is_first, moved_flags.reshape(slot_count), out_flags)
        else:
            out_rows, out_flags, values = later_segment()
        if tick_index < round_total + segment_count - 2:
            carried, carried_flags = shifted((out_rows, out_flags), "segment", 1)
        updated = lax.dynamic_update_index_in_dim(results, values, query_pass_portion, 0)
        results = jnp.where(is_live, updated, results)
    return results[None]


def solution(mesh):
    placed = (
        P(None, "shard", None),
        P(None, "shard", None),
        P(None, "shard"),
        P(None, "shard"),
        P(None, "shard", None),
        P("shard", None),
        P(),
        P(),
        P(),
        P(None, "shard", None),
        P(None, "shard", None),
        P(),
        P(),
    )
    return jax.shard_map(
        local, mesh=mesh, in_specs=placed, out_specs=P("segment", None, "shard"), check_vma=False
    )
```

profile of v0, /device:TPU:1, one launch (start us, length us, event | category | flops | bytes accessed | tf_op | source)
XLA Modules:
  0.0 542.7 jit_solution(366010072755618632)
XLA Ops:
  6.5 0.7 copy-done
  7.9 1.3 constant_dynamic-slice_fusion.12
  9.3 0.7 convert_element_type.192
  11.0 1.4 constant_dynamic-slice_fusion.6
  12.4 2.1 compare_convert_fusion
  14.7 0.9 constant_dynamic-slice_fusion.10
  15.7 79.9 %all-gather.3.cloned.1.call-done = bf16[1,4096,128]{2,1,0:T(8,128)(2,1)} async-done(((bf16[1,32,128]{2,1,0:T(8,128)(2,1)}), bf16[1,4096,128]{2,1,0:T(8,128)(2,1)}) %all-gather.3.cloned.1.call-update) | async-done | bytes 1048592 | tf_op jit(solution)/shard_map/all_gather | solution.py:91
  95.6 78.0 %all-gather.5.cloned.1.call-done = bf16[1,4096,128]{2,1,0:T(8,128)(2,1)} async-done(((bf16[1,32,128]{2,1,0:T(8,128)(2,1)}), bf16[1,4096,128]{2,1,0:T(8,128)(2,1)}) %all-gather.5.cloned.1.call-update) | async-done | bytes 1048592 | tf_op jit(solution)/shard_map/all_gather | solution.py:92
  173.5 14.3 %conditional.2 = (bf16[256]{0:T(256)(128)(2,1)S(1)}, f32[1,256]{1,0:T(1,128)S(1)}, bf16[256,4096]{1,0:T(8,128)(2,1)}, bf16[128,2,4096]{2,1,0:T(2,128)(2,1)S(1)}) conditional(s32[]{:T(128)} %convert_element_type.164, (pred[]{:T(512)}, f32[4096]{0:T(1024)S(1)}, bf16[4096,128]{1,0:T(8,128)(2,1)}, bf16[4096,128]{1,0:T(8,128)(2,1)}, f32[4096]{0:T(1024)S(1)}, ...), branch_computations={%region_2.4_spmd, %region_4.7_spmd} | conditional | flops 1347585536 | bytes 14966350 | solution.py:160
  174.2 3.3 fusion.31
  177.6 1.3 gather_fusion
  179.7 2.0 fusion.29
  181.7 3.0 copy.41
  184.7 3.2 reshape.110
  187.9 59.4 %all_to_all.30 = bf16[128,2,4096]{2,1,0:T(2,128)(2,1)} all-to-all(bf16[128,2,4096]{2,1,0:T(2,128)(2,1)S(1)} %get-tuple-element.142), channel_id=1, replica_groups=mesh['segment'=4,'shard'=128] {'shard'}, dimensions={0} | all-to-all | bytes 4194304 | tf_op jit(solution)/shard_map/all_to_all | solution.py:162
  247.3 2.7 reshape.77
  250.1 1.6 broadcast_select_fusion.1
  251.6 1.4 collective-permute-start
  253.4 0.8 all_to_all.24
  254.2 8.9 %all-to-all-start.1 = ((bf16[128,1,2]{2,1,0:T(2,128)(2,1)}), bf16[128,1,2]{2,1,0:T(2,128)(2,1)S(1)}, u32[]{:S(2)}, u32[]{:S(2)}) async-start(bf16[128,1,2]{2,1,0:T(2,128)(2,1)} %all_to_all.24), calls=%async_computation.1 | async-start | bytes 131072 | tf_op jit(solution)/shard_map/all_to_all | solution.py:169
  263.1 11.4 %all-to-all-done.1 = bf16[128,1,2]{2,1,0:T(2,128)(2,1)S(1)} async-done(((bf16[128,1,2]{2,1,0:T(2,128)(2,1)}), bf16[128,1,2]{2,1,0:T(2,128)(2,1)S(1)}, u32[]{:S(2)}, u32[]{:S(2)}) %all-to-all-start.1) | async-done | bytes 544 | tf_op jit(solution)/shard_map/all_to_all | solution.py:169
  274.9 1.3 collective-permute-start.1
  276.2 20.0 %collective-permute-done.1 = bf16[256]{0:T(256)(128)(2,1)S(1)} collective-permute-done((bf16[256]{0:T(256)(128)(2,1)S(1)}, bf16[256]{0:T(256)(128)(2,1)S(1)}, u32[]{:S(2)}, u32[]{:S(2)}) %collective-permute-start.1) | collective-permute-done | bytes 544 | tf_op jit(solution)/shard_map/ppermute | solution.py:10
  296.2 13.9 %conditional.3 = (bf16[256]{0:T(256)(128)(2,1)S(1)}, f32[1,256]{1,0:T(1,128)S(1)}, bf16[256,4096]{1,0:T(8,128)(2,1)}, bf16[128,2,4096]{2,1,0:T(2,128)(2,1)S(1)}) conditional(s32[]{:T(128)} %convert_element_type.164, (pred[]{:T(512)}, bf16[256,4096]{1,0:T(8,128)(2,1)S(1)}, f32[4096]{0:T(1024)S(1)}, bf16[4096,128]{1,0:T(8,128)(2,1)S(1)}, ...), branch_computations={%region_9.11_spmd, %region_11.14_spmd} | conditional | flops 1347585536 | bytes 14966350 | solution.py:160
  296.4 3.4 fusion.49
  299.8 1.3 gather_fusion.1
  301.1 0.7 compare_select_fusion.3
  302.0 2.0 fusion.47
  304.0 3.0 copy.43
  307.0 3.2 reshape.112
  310.2 62.4 %all_to_all.31 = bf16[128,2,4096]{2,1,0:T(2,128)(2,1)} all-to-all(bf16[128,2,4096]{2,1,0:T(2,128)(2,1)S(1)} %get-tuple-element.144), channel_id=1, replica_groups=mesh['segment'=4,'shard'=128] {'shard'}, dimensions={0} | all-to-all | bytes 4194304 | tf_op jit(solution)/shard_map/all_to_all | solution.py:162
  372.6 2.7 reshape.80
  375.4 1.8 broadcast_select_fusion
  377.1 1.4 collective-permute-start.2
  378.7 20.1 %all_to_all.32 = bf16[128,1,2]{2,1,0:T(2,128)(2,1)S(1)} all-to-all(bf16[128,1,2]{2,1,0:T(2,128)(2,1)S(1)} %all_to_all.25), channel_id=1, replica_groups=mesh['segment'=4,'shard'=128] {'shard'}, dimensions={0} | all-to-all | bytes 1024 | tf_op jit(solution)/shard_map/all_to_all | solution.py:169
  399.2 1.5 collective-permute-start.3
  400.7 21.0 %collective-permute-done.3 = bf16[256]{0:T(256)(128)(2,1)S(1)} collective-permute-done((bf16[256]{0:T(256)(128)(2,1)S(1)}, bf16[256]{0:T(256)(128)(2,1)S(1)}, u32[]{:S(2)}, u32[]{:S(2)}) %collective-permute-start.3) | collective-permute-done | bytes 544 | tf_op jit(solution)/shard_map/ppermute | solution.py:10
  421.7 6.0 %fusion.77 = (bf16[256,4096]{1,0:T(8,128)(2,1)}, f32[256,4096]{1,0:T(8,128)}) fusion(f32[256]{0:T(256)S(1)} %convert_element_type.177, pred[]{:T(512)} %eq.29, bf16[256,4096]{1,0:T(8,128)(2,1)S(1)} %collective-permute-done.2, f32[4096]{0:T(1024)S(1)} %bitcast.94, f32[4096]{0:T(1024)S(1)} %bitcast.104, ...), kind=kOutput, calls=%fused_computation.97 | convolution fusion | flops 552697856 | bytes 10519553 | tf_op jit(solution)/shard_map/dot_general | solution.py:53
  427.7 4.1 collective-permute-start.4
  431.9 1.8 collective-permute-start.5
  433.6 40.4 %collective-permute-done.5 = bf16[256]{0:T(256)(128)(2,1)S(1)} collective-permute-done((bf16[256]{0:T(256)(128)(2,1)S(1)}, bf16[256]{0:T(256)(128)(2,1)S(1)}, u32[]{:S(2)}, u32[]{:S(2)}) %collective-permute-start.5) | collective-permute-done | bytes 544 | tf_op jit(solution)/shard_map/ppermute | solution.py:10
  474.0 1.3 copy-done.3
  475.4 10.1 %multiply_reduce_fusion.6 = (f32[256]{0:T(256)S(1)}, f32[256]{0:T(256)S(1)}, bf16[256,4096]{1,0:T(8,128)(2,1)}) fusion(f32[256]{0:T(256)S(1)} %convert_element_type.183, f32[4096]{0:T(1024)S(1)} %bitcast.99, pred[]{:T(512)} %eq.29, bf16[256,4096]{1,0:T(8,128)(2,1)} %copy-done.3, f32[4096]{0:T(1024)S(1)} %bitcast.95, f32[256]{0:T(256)S(1)} %convert_element_type.177, ...), kind=kOutput, calls=%fused_computation.89 | convolution fusion | flops 566328832 | bytes 12636161 | tf_op jit(solution)/shard_map/dot_general | solution.py:53
  485.5 4.1 collective-permute-start.6
  489.7 2.1 collective-permute-start.7
  491.8 39.0 %collective-permute-done.7 = bf16[256]{0:T(256)(128)(2,1)S(1)} collective-permute-done((bf16[256]{0:T(256)(128)(2,1)S(1)}, bf16[256]{0:T(256)(128)(2,1)S(1)}, u32[]{:S(2)}, u32[]{:S(2)}) %collective-permute-start.7) | collective-permute-done | bytes 544 | tf_op jit(solution)/shard_map/ppermute | solution.py:10
  530.9 3.6 fusion.72
  534.6 1.3 select_n.227
  (58 shorter events, 5.0 us)
Async XLA Ops:
  6.5 0.7 copy-start
  6.5 89.0 %all-gather.3.cloned.1.call-start = ((), (), s32[]{:S(2)}) async-start(), calls=%async_computation.4 | async-start | bytes 1056768 | tf_op jit(solution)/shard_map/all_gather | solution.py:91
  7.9 165.7 %all-gather.5.cloned.1.call-start = ((), (), s32[]{:S(2)}) async-start(), calls=%async_computation.5 | async-start | bytes 1056768 | tf_op jit(solution)/shard_map/all_gather | solution.py:92
  250.0 46.2 %copy-start.2 = (bf16[1024]{0:T(1024)(128)(2,1)S(1)}, bf16[1024]{0:T(1024)(128)(2,1)}, u32[]{:S(2)}) copy-start(bf16[1024]{0:T(1024)(128)(2,1)} %param.25) | copy-start | bytes 6148
  250.0 46.2 %copy-start.4 = (bf16[1,4096,128]{2,1,0:T(8,128)(2,1)S(1)}, bf16[1,4096,128]{2,1,0:T(8,128)(2,1)}, u32[]{:S(2)}) copy-start(bf16[1,4096,128]{2,1,0:T(8,128)(2,1)} %all-gather.3.cloned.1.call-done) | copy-start | bytes 3145732
  250.0 46.2 %copy-start.5 = (f32[1024]{0:T(1024)S(1)}, f32[1024]{0:T(1024)}, u32[]{:S(2)}) copy-start(f32[1024]{0:T(1024)} %param.24) | copy-start | bytes 12292
  251.6 44.6 %collective-permute-start = (bf16[256,4096]{1,0:T(8,128)(2,1)}, bf16[256,4096]{1,0:T(8,128)(2,1)S(1)}, u32[]{:S(2)}, u32[]{:S(2)}) collective-permute-start(bf16[256,4096]{1,0:T(8,128)(2,1)} %broadcast_select_fusion.1), channel_id=1, source_target_pairs={{0,128},{128,256},{256,384},{1,129},{129,257},{257,385},{2,130},{1... | collective-permute-start | bytes 6291464 | tf_op jit(solution)/shard_map/ppermute | solution.py:10
  254.2 20.3 %all-to-all-start.1 = ((bf16[128,1,2]{2,1,0:T(2,128)(2,1)}), bf16[128,1,2]{2,1,0:T(2,128)(2,1)S(1)}, u32[]{:S(2)}, u32[]{:S(2)}) async-start(bf16[128,1,2]{2,1,0:T(2,128)(2,1)} %all_to_all.24), calls=%async_computation.1 | async-start | bytes 131072 | tf_op jit(solution)/shard_map/all_to_all | solution.py:169
  274.9 21.4 %collective-permute-start.1 = (bf16[256]{0:T(256)(128)(2,1)S(1)}, bf16[256]{0:T(256)(128)(2,1)S(1)}, u32[]{:S(2)}, u32[]{:S(2)}) collective-permute-start(bf16[256]{0:T(256)(128)(2,1)S(1)} %broadcast_select_fusion.8), channel_id=1, source_target_pairs={{0,128},{128,256},{256,384},{1,129},{129,257},{257,385},{2,130},{1... | collective-permute-start | bytes 1544 | tf_op jit(solution)/shard_map/ppermute | solution.py:10
  377.1 44.6 %collective-permute-start.2 = (bf16[256,4096]{1,0:T(8,128)(2,1)}, bf16[256,4096]{1,0:T(8,128)(2,1)S(1)}, u32[]{:S(2)}, u32[]{:S(2)}) collective-permute-start(bf16[256,4096]{1,0:T(8,128)(2,1)} %broadcast_select_fusion), channel_id=1, source_target_pairs={{0,128},{128,256},{256,384},{1,129},{129,257},{257,385},{2,130},{1... | collective-permute-start | bytes 6291464 | tf_op jit(solution)/shard_map/ppermute | solution.py:10
  399.2 22.5 %collective-permute-start.3 = (bf16[256]{0:T(256)(128)(2,1)S(1)}, bf16[256]{0:T(256)(128)(2,1)S(1)}, u32[]{:S(2)}, u32[]{:S(2)}) collective-permute-start(bf16[256]{0:T(256)(128)(2,1)S(1)} %broadcast_select_fusion.7), channel_id=1, source_target_pairs={{0,128},{128,256},{256,384},{1,129},{129,257},{257,385},{2,130},{1... | collective-permute-start | bytes 1544 | tf_op jit(solution)/shard_map/ppermute | solution.py:10
  427.7 46.3 %collective-permute-start.4 = (bf16[256,4096]{1,0:T(8,128)(2,1)}, bf16[256,4096]{1,0:T(8,128)(2,1)S(1)}, u32[]{:S(2)}, u32[]{:S(2)}) collective-permute-start(bf16[256,4096]{1,0:T(8,128)(2,1)} %get-tuple-element.168), channel_id=1, source_target_pairs={{0,128},{128,256},{256,384},{1,129},{129,257},{257,385},{2,130},{1... | collective-permute-start | bytes 6291464 | tf_op jit(solution)/shard_map/ppermute | solution.py:10
  431.9 42.2 %collective-permute-start.5 = (bf16[256]{0:T(256)(128)(2,1)S(1)}, bf16[256]{0:T(256)(128)(2,1)S(1)}, u32[]{:S(2)}, u32[]{:S(2)}) collective-permute-start(bf16[256]{0:T(256)(128)(2,1)S(1)} %collective-permute-done.3), channel_id=1, source_target_pairs={{0,128},{128,256},{256,384},{1,129},{129,257},{257,385},{2,130},{1... | collective-permute-start | bytes 1544 | tf_op jit(solution)/shard_map/ppermute | solution.py:10
  474.0 1.3 copy-start.3
  485.5 45.4 %collective-permute-start.6 = (bf16[256,4096]{1,0:T(8,128)(2,1)}, bf16[256,4096]{1,0:T(8,128)(2,1)S(1)}, u32[]{:S(2)}, u32[]{:S(2)}) collective-permute-start(bf16[256,4096]{1,0:T(8,128)(2,1)} %get-tuple-element.161), channel_id=1, source_target_pairs={{0,128},{128,256},{256,384},{1,129},{129,257},{257,385},{2,130},{1... | collective-permute-start | bytes 6291464 | tf_op jit(solution)/shard_map/ppermute | solution.py:10
  489.7 41.1 %collective-permute-start.7 = (bf16[256]{0:T(256)(128)(2,1)S(1)}, bf16[256]{0:T(256)(128)(2,1)S(1)}, u32[]{:S(2)}, u32[]{:S(2)}) collective-permute-start(bf16[256]{0:T(256)(128)(2,1)S(1)} %collective-permute-done.5), channel_id=1, source_target_pairs={{0,128},{128,256},{256,384},{1,129},{129,257},{257,385},{2,130},{1... | collective-permute-start | bytes 1544 | tf_op jit(solution)/shard_map/ppermute | solution.py:10
  530.9 3.6 copy-start.1
Sparse Core Ops, SparseCore 0:
  10.4 85.1 all-gather.2
  98.6 74.8 all-gather.4
where the time goes:
time: 552 us; the launch traced here: 543 us
  waiting for transfers between devices  290 us (53%)
  blocking collectives  142 us (26%)
  local copies, waits for them, and re-layouts  30.7 us (6%)
  matrix products  30.5 us (6%)
  starting transfers between devices  26.6 us (5%)
  between operations  13.7 us (2%)
  other arithmetic  9.23 us (2%)
    all_to_all x2, blocking collectives, local(): lax.all_to_all(out_rows.reshape(shard_count, cap_slots, vector_length), '...  122 us
    ppermute x8, waiting for transfers between devices, shifted(): return lax.ppermute(value, axis, pairs)  120 us
    all_gather x1, waiting for transfers between devices, local(): lax.all_gather(up_local, 'shard', axis=1, tiled=True)  79.9 us
    all_gather x1, waiting for transfers between devices, local(): lax.all_gather(back_local, 'shard', axis=1, tiled=True)  78 us
    all_to_all x1, blocking collectives, local(): lax.all_to_all(out_flags.reshape(shard_count, cap_slots), 'shard', split_...  20.1 us
    dot_general x3, matrix products, rank_section(): lax.dot_general(active, back_weight, (((1,), (1,)), ((), ())), preferred_...  19.8 us
    ppermute x8, starting transfers between devices, shifted(): return lax.ppermute(value, axis, pairs)  17.7 us
    all_to_all x1, waiting for transfers between devices, local(): lax.all_to_all(out_flags.reshape(shard_count, cap_slots), 'shard', split_...  11.4 us
  transfers between devices with their start and end apart: 11, of which 7 were waited for; matrix products, arithmetic and copies ran while one was open for 2% of the time, Pallas kernels for 0%

commit v1 on v0

v1 whole, which is shorter than its diff:
```python
import jax
import jax.numpy as jnp
from jax import lax
from jax.sharding import PartitionSpec as P

F32 = jnp.float32
BF16 = jnp.bfloat16
HIGH = lax.Precision.HIGHEST
LANES = 128


def fdot(a, b, precision=None):
    return jnp.dot(a, b, preferred_element_type=F32, precision=precision)


def gather_blocks(block):
    return lax.all_gather(block, "shard", axis=0, tiled=False)


def sum_segments(value):
    return lax.psum(value, "segment")


def local(
    proposal_attributes,
    keeper_ordering_vectors,
    keeper_positions,
    alive_tallies,
    holder_shards,
    holder_attribute_factor,
    early_inner_matrix,
    early_inner_offset,
    early_grading_vector,
    block_lowering_matrices,
    block_raising_flipped,
    block_result_offsets,
    block_grading_vectors,
):
    segment_id = lax.axis_index("segment")
    segment_count = lax.axis_size("segment")
    shard_count = lax.axis_size("shard")
    rounds, entries, width = keeper_ordering_vectors.shape
    candidates = proposal_attributes.shape[1]
    low_rank = block_lowering_matrices.shape[2]
    cap_slots = max(2, 2 * entries // shard_count)
    rows = rounds * entries
    own_features = width // shard_count
    piece = own_features // segment_count
    part_width = width // segment_count
    span = segment_count * LANES
    spans = width // span

    at = lax.broadcasted_iota(jnp.int32, (span, LANES), 0)
    to = lax.broadcasted_iota(jnp.int32, (span, LANES), 1)
    chosen = (at // own_features == to // piece) & (
        at % own_features == segment_id * piece + to % piece
    )
    pick = chosen.astype(BF16)
    pick32 = chosen.astype(F32)

    def part_of(values):
        return [fdot(values[:, g * span : (g + 1) * span], pick) for g in range(spans)]

    def part_of32(values):
        return jnp.concatenate(
            [fdot(values[:, g * span : (g + 1) * span], pick32, HIGH) for g in range(spans)], 1
        )

    own_gain = jnp.concatenate(part_of(holder_attribute_factor), 0).astype(BF16)
    own_lower = lax.dynamic_slice_in_dim(block_lowering_matrices, segment_id * piece, piece, 1)
    own_raise = lax.dynamic_slice_in_dim(block_raising_flipped, segment_id * piece, piece, 1)
    block = jnp.concatenate(
        [own_lower.reshape(3 * piece, low_rank), own_raise.reshape(3 * piece, low_rank), own_gain], 0
    )
    blocks = gather_blocks(block)

    def matrix(k):
        return blocks[:, k * piece : (k + 1) * piece].reshape(part_width, low_rank)

    hidden = jax.nn.relu(
        fdot(proposal_attributes.reshape(rounds * candidates, -1), early_inner_matrix)
        + early_inner_offset
    ).astype(BF16)
    scores = fdot(hidden, early_grading_vector).reshape(rounds, candidates)
    ids = jnp.arange(candidates, dtype=jnp.int32)
    looked_up = jnp.sum(
        jnp.where(keeper_positions[:, :, None] == ids, scores[:, None, :], 0.0), axis=2
    )
    keep = (keeper_positions < alive_tallies).astype(F32)
    gate = jax.nn.sigmoid(looked_up) * keep

    owner = holder_shards[:, :, 0]
    order = jnp.arange(entries, dtype=jnp.int32)
    same = (owner[:, :, None] == owner[:, None, :]) & (order[None, :] < order[:, None])
    within = jnp.sum(same.astype(jnp.int32), axis=2)
    target = owner * cap_slots + within
    slots = jnp.arange(shard_count * cap_slots, dtype=jnp.int32)
    placed = slots[None, :, None] == target[:, None, :]

    gate_col = gate.reshape(rows, 1)
    keep_col = keep.reshape(rows, 1)
    own_rows = jnp.concatenate(part_of(keeper_ordering_vectors.reshape(rows, width)), 1)
    h0 = (own_rows * gate_col).astype(BF16)
    owner_hot = (
        owner.reshape(rows, 1) == jnp.arange(shard_count, dtype=jnp.int32)[None, :]
    ).astype(BF16)
    gains = jnp.concatenate(
        [fdot(owner_hot, blocks[:, 6 * piece + g]) for g in range(part_width // LANES)], 1
    )
    x = (h0.astype(F32) * gains).astype(BF16)

    biases = part_of32(block_result_offsets)
    heads = part_of32(block_grading_vectors)
    lower1, lower2, lower3, raise1, raise2, raise3 = [matrix(k) for k in range(6)]

    between = lax.dot_general(
        raise2, lower3, (((0,), (0,)), ((), ())), preferred_element_type=F32
    )
    raised = lax.dot_general(
        heads[1:3], raise2.astype(F32), (((1,), (0,)), ((), ())), precision=HIGH
    )
    raised3 = lax.dot_general(
        heads[2:3], raise3.astype(F32), (((1,), (0,)), ((), ())), precision=HIGH
    )
    lowered_bias = lax.dot_general(
        biases[1:2], lower3.astype(F32), (((1,), (0,)), ((), ())), precision=HIGH
    )
    consts = jnp.stack(
        [
            jnp.sum(biases[1] * heads[1]),
            jnp.sum(biases[1] * heads[2]),
            jnp.sum(biases[2] * heads[2]),
        ]
    )
    consts = jnp.pad(consts, (0, low_rank - 3))[None]
    first = jnp.concatenate(
        [fdot(x, lower1), between, raised, raised3, lowered_bias, consts], 0
    )
    first = sum_segments(jnp.pad(first, ((0, 3), (0, 0))))

    act1 = first[:rows].astype(BF16)
    lifted = (
        lax.dot_general(act1, raise1, (((1,), (1,)), ((), ())), preferred_element_type=F32)
        + biases[0]
    )
    x32 = x.astype(F32)
    out1 = (x32 + x32 * lifted) * keep_col
    h1 = out1.astype(BF16)
    h1_32 = h1.astype(F32)
    graded = jnp.stack(
        [
            jnp.sum(out1 * heads[0], axis=1),
            jnp.sum(h1_32 * heads[1], axis=1),
            jnp.sum(h1_32 * heads[2], axis=1),
        ]
    ).reshape(-1, low_rank)
    second = jnp.concatenate([fdot(h1, lower2), fdot(h1, lower3), graded], 0)
    second = sum_segments(jnp.pad(second, ((0, -second.shape[0] % 8), (0, 0))))

    between = first[rows : rows + low_rank]
    vectors = first[rows + low_rank : rows + low_rank + 5]
    graded = second[2 * rows : 2 * rows + 3 * rows // low_rank].reshape(3, rows)
    keep_row = keep.reshape(rows)
    act2 = jax.nn.relu(second[:rows]).astype(BF16).astype(F32)
    graded2 = graded[1] + jnp.sum(act2 * vectors[0], axis=1) + vectors[4, 0]
    inner3 = (second[rows : 2 * rows] + fdot(act2, between, HIGH) + vectors[3]) * keep_col
    act3 = jax.nn.relu(inner3).astype(BF16).astype(F32)
    graded3 = (
        (graded[2] + jnp.sum(act2 * vectors[1], axis=1) + vectors[4, 1]) * keep_row
        + jnp.sum(act3 * vectors[2], axis=1)
        + vectors[4, 2]
    )
    section = jnp.stack([gate.reshape(rows), graded[0], graded2 * keep_row, graded3 * keep_row])
    values = lax.dynamic_index_in_dim(section, segment_id, 0, keepdims=False)
    values = values.reshape(rounds, 1, entries)
    sent = jnp.sum(jnp.where(placed, values, 0.0), axis=2)
    outgoing = sent.reshape(rounds, shard_count, cap_slots).transpose(1, 0, 2)
    outgoing = outgoing.reshape(shard_count, rounds * cap_slots)
    arrived = lax.all_to_all(outgoing, "shard", split_axis=0, concat_axis=0, tiled=True)
    arrived = arrived.reshape(shard_count, rounds, cap_slots).transpose(1, 0, 2)
    arrived = arrived.reshape(rounds, shard_count * cap_slots)
    return jnp.where(segment_id == 0, sent, arrived)[None]


def solution(mesh):
    placed = (
        P(None, "shard", None),
        P(None, "shard", None),
        P(None, "shard"),
        P(None, "shard"),
        P(None, "shard", None),
        P("shard", None),
        P(),
        P(),
        P(),
        P(None, "shard", None),
        P(None, "shard", None),
        P(),
        P(),
    )
    return jax.shard_map(
        local, mesh=mesh, in_specs=placed, out_specs=P("segment", None, "shard"), check_vma=False
    )
```

time: 552 us -> 262 us (0.47); the launches traced: 543 us -> 261 us
  blocking collectives: 142 us -> 0 us
  waiting for transfers between devices: 290 us -> 164 us
  local copies, waits for them, and re-layouts: 30.7 us -> 12.4 us
  matrix products: 30.5 us -> 45.1 us
  starting transfers between devices: 26.6 us -> 16.4 us
    all_to_all x3 -> x0, blocking collectives: 142 us -> none  [the longest x2 122 us: local(): lax.all_to_all(out_rows.reshape(shard_count, cap_slots, vector_length), '...]
    ppermute x8 -> x0, waiting for transfers between devices: 120 us -> none  [shifted(): return lax.ppermute(value, axis, pairs)]
    all_gather x2 -> x1, waiting for transfers between devices: 158 us -> 55.1 us  [gather_blocks(): return lax.all_gather(block, 'shard', axis=0, tiled=False)]
    psum x0 -> x2, waiting for transfers between devices: none -> 97.2 us  [sum_segments(): return lax.psum(value, 'segment')]
    ppermute x8 -> x0, starting transfers between devices: 17.7 us -> none  [shifted(): return lax.ppermute(value, axis, pairs)]
    dot_general x7 -> x50, matrix products: 30.5 us -> 45.2 us  [the longest x45 42.6 us: fdot(): return jnp.dot(a, b, preferred_element_type=F32, precision=precision)]
    reshape x6 -> x4, local copies, waits for them, and re-layouts: 12.1 us -> 1.01 us  [the longest x1 0.71 us: local(): own_raise.reshape(3 * piece, low_rank)]
    all_to_all x1, starting transfers between devices: 8.85 us -> 16.3 us  [local(): lax.all_to_all(outgoing, 'shard', split_axis=0, concat_axis=0, tiled=True)]
  transfers between devices with their start and end apart: 11 -> 4, of which waited for: 7 -> 4; matrix products, arithmetic and copies ran while one was open for 2% -> 14% of each run, Pallas kernels for 0% -> 0%
where the time goes in v1:
time: 262 us; the launch traced here: 261 us
  waiting for transfers between devices  164 us (63%)
  matrix products  45.1 us (17%)
  starting transfers between devices  16.4 us (6%)
  between operations  13.4 us (5%)
  local copies, waits for them, and re-layouts  12.4 us (5%)
  other arithmetic  9.7 us (4%)
    psum x2, waiting for transfers between devices, sum_segments(): return lax.psum(value, 'segment')  97.2 us
    all_gather x1, waiting for transfers between devices, gather_blocks(): return lax.all_gather(block, 'shard', axis=0, tiled=False)  55.1 us
    dot_general x45, matrix products, fdot(): return jnp.dot(a, b, preferred_element_type=F32, precision=precision)  42.6 us
    all_to_all x1, starting transfers between devices, local(): lax.all_to_all(outgoing, 'shard', split_axis=0, concat_axis=0, tiled=True)  16.3 us
    all_to_all x1, waiting for transfers between devices, local(): lax.all_to_all(outgoing, 'shard', split_axis=0, concat_axis=0, tiled=True)  11.4 us
  transfers between devices with their start and end apart: 4, of which 4 were waited for; matrix products, arithmetic and copies ran while one was open for 14% of the time, Pallas kernels for 0%

profile of v1, /device:TPU:1, one launch (start us, length us, event | category | flops | bytes accessed | tf_op | source)
XLA Modules:
  0.0 260.8 jit_solution(11579320052899533610)
XLA Ops:
  7.3 0.8 fusion.38
  8.1 0.8 fusion.40
  8.9 0.8 fusion.42
  9.7 0.8 fusion.44
  10.6 0.8 fusion.46
  11.4 0.8 fusion.48
  14.6 1.8 concatenate.25
  17.2 0.9 fusion.28
  18.0 0.9 fusion.27
  18.9 0.9 fusion.26
  19.8 0.9 fusion.25
  20.7 0.9 fusion.24
  21.6 0.9 fusion.23
  22.5 0.9 fusion.22
  23.4 0.9 fusion.21
  24.3 0.9 fusion.36
  25.1 0.9 fusion.35
  26.0 0.9 fusion.34
  26.9 0.9 fusion.33
  27.8 0.9 fusion.32
  28.7 0.9 fusion.31
  29.6 4.4 %fusion = f32[1,1024]{1,0:T(1,128)S(1)} fusion(bf16[1024,1]{0,1:T(2,128)(2,1)S(1)} %reshape.249, f32[1024]{0:T(1024)} %param.20, bf16[1024,1024]{1,0:T(8,128)(2,1)S(1)} %bitcast.325, bf16[1024,1024]{1,0:T(8,128)(2,1)} %param.19), kind=kOutput, calls=%fused_computation.1 | convolution fusion | flops 2152726528 | bytes 4204544 | tf_op jit(solution)/shard_map/dot_general | solution.py:13
  34.2 1.0 fusion.30
  35.2 0.9 fusion.29
  36.8 2.0 fusion.155
  39.2 1.8 fusion.13
  41.0 1.8 fusion.12
  42.9 1.8 fusion.11
  44.7 1.8 fusion.10
  46.6 0.9 fusion.9
  47.4 0.9 fusion.8
  48.3 0.9 fusion.7
  49.2 0.9 fusion.6
  50.1 55.1 %all-gather.3.cloned.1.call-done = bf16[7168,128]{1,0:T(8,128)(2,1)} async-done(((bf16[56,128]{1,0:T(8,128)(2,1)}), bf16[7168,128]{1,0:T(8,128)(2,1)}) %all-gather.3.cloned.1.call-update) | async-done | bytes 1835024 | tf_op jit(solution)/shard_map/all_gather | solution.py:17
  105.2 2.9 %fusion.164 = (bf16[128,1,128]{2,1,0:T(2,128)(2,1)S(1)}, bf16[128,1,128]{2,1,0:T(2,128)(2,1)S(1)}, bf16[128,1,128]{2,1,0:T(2,128)(2,1)S(1)}, bf16[128,1,128]{2,1...) fusion(bf16[128,56,128]{2,1,0:T(8,128)(2,1)} %bitcast.326), kind=kLoop, calls=%fused_computation.267 | loop fusion | bytes 524288 | tf_op jit(solution)/shard_map/slice | solution.py:108
  108.2 1.1 fusion.163
  112.1 1.4 multiply_convert_fusion
  114.9 46.5 %all-reduce.6.cloned.1.call-done = f32[392,128]{1,0:T(8,128)} async-done(((f32[392,128]{1,0:T(8,128)}), f32[392,128]{1,0:T(8,128)}) %all-reduce.6.cloned.1.call-update) | async-done | bytes 200720 | tf_op jit(solution)/shard_map/psum | solution.py:21
  161.4 1.7 fusion.53
  163.1 1.3 fusion.63
  164.4 1.3 fusion.76
  166.4 1.4 fusion.166
  168.7 50.7 %all-reduce.8.cloned.1.call-done = f32[520,128]{1,0:T(8,128)} async-done(((f32[520,128]{1,0:T(8,128)}), f32[520,128]{1,0:T(8,128)}) %all-reduce.8.cloned.1.call-update) | async-done | bytes 266256 | tf_op jit(solution)/shard_map/psum | solution.py:21
  220.2 1.3 fusion.20
  221.5 1.1 fusion.83
  222.5 1.9 add_multiply_fusion.1
  225.6 16.3 %all-to-all-start = ((f32[128,1,4]{2,1,0:T(1,128)}), f32[128,1,4]{2,1,0:T(1,128)S(1)}, u32[]{:S(2)}, u32[]{:S(2)}) async-start(f32[128,1,4]{2,1,0:T(1,128)} %copy.50), calls=%async_computation | async-start | bytes 131072 | tf_op jit(solution)/shard_map/all_to_all | solution.py:179
  241.9 11.4 %all-to-all-done = f32[128,1,4]{2,1,0:T(1,128)S(1)} async-done(((f32[128,1,4]{2,1,0:T(1,128)}), f32[128,1,4]{2,1,0:T(1,128)S(1)}, u32[]{:S(2)}, u32[]{:S(2)}) %all-to-all-start) | async-done | bytes 2080 | tf_op jit(solution)/shard_map/all_to_all | solution.py:179
  (69 shorter events, 13.6 us)
Async XLA Ops:
  6.5 23.1 %copy-start = (bf16[2,512,1024]{2,1,0:T(8,128)(2,1)S(1)}, bf16[2,512,1024]{2,1,0:T(8,128)(2,1)}, u32[]{:S(2)}) copy-start(bf16[2,512,1024]{2,1,0:T(8,128)(2,1)} %param.13) | copy-start | bytes 6291460
  6.5 98.7 %all-gather.3.cloned.1.call-start = ((), (), s32[]{:S(2)}) async-start(), calls=%async_computation.3 | async-start | bytes 1849344 | tf_op jit(solution)/shard_map/all_gather | solution.py:17
  16.4 144.9 %all-reduce.6.cloned.1.call-start = ((), (), s32[]{:S(2)}) async-start(), calls=%async_computation.1 | async-start | bytes 401408 | tf_op jit(solution)/shard_map/psum | solution.py:21
  29.6 4.4 %copy-start.3 = (s32[2,128]{1,0:T(2,128)S(1)}, s32[2,128]{1,0:T(2,128)}, u32[]{:S(2)}) copy-start(s32[2,128]{1,0:T(2,128)} %param.15) | copy-start | bytes 3076
  29.6 4.4 %copy-start.4 = (s32[2,1]{0,1:T(1,128)S(1)}, s32[2,1]{0,1:T(1,128)}, u32[]{:S(2)}) copy-start(s32[2,1]{0,1:T(1,128)} %param.16) | copy-start | bytes 28
  29.6 9.2 %copy-start.2 = (s32[2,128,1]{1,2,0:T(1,128)S(1)}, s32[2,128,1]{1,2,0:T(1,128)}, u32[]{:S(2)}) copy-start(s32[2,128,1]{1,2,0:T(1,128)} %param.17) | copy-start | bytes 3076
  34.1 12.4 %copy-start.5 = (bf16[2,128,4096]{2,1,0:T(8,128)(2,1)S(1)}, bf16[2,128,4096]{2,1,0:T(8,128)(2,1)}, u32[]{:S(2)}) copy-start(bf16[2,128,4096]{2,1,0:T(8,128)(2,1)} %param.14) | copy-start | bytes 6291460
  105.2 4.0 %copy-start.1 = (bf16[7168,128]{1,0:T(8,128)(2,1)S(1)}, bf16[7168,128]{1,0:T(8,128)(2,1)}, u32[]{:S(2)}) copy-start(bf16[7168,128]{1,0:T(8,128)(2,1)} %all-gather.3.cloned.1.call-done) | copy-start | bytes 5505028
  114.9 104.5 %all-reduce.8.cloned.1.call-start = ((), (), s32[]{:S(2)}) async-start(), calls=%async_computation.2 | async-start | bytes 532480 | tf_op jit(solution)/shard_map/psum | solution.py:21
  225.6 27.7 %all-to-all-start = ((f32[128,1,4]{2,1,0:T(1,128)}), f32[128,1,4]{2,1,0:T(1,128)S(1)}, u32[]{:S(2)}, u32[]{:S(2)}) async-start(f32[128,1,4]{2,1,0:T(1,128)} %copy.50), calls=%async_computation | async-start | bytes 131072 | tf_op jit(solution)/shard_map/all_to_all | solution.py:179
Sparse Core Ops, SparseCore 0:
  16.6 88.6 all-gather.2
  115.0 46.3 all-reduce.5
  166.5 52.7 all-reduce.7

commit v2 on v1

--- a/solution.py
+++ b/solution.py
@@ -1,6 +1,11 @@
+import functools
+import math
+
 import jax
 import jax.numpy as jnp
 from jax import lax
+from jax.experimental import pallas as pl
+from jax.experimental.pallas import tpu as pltpu
 from jax.sharding import PartitionSpec as P
 
 F32 = jnp.float32
@@ -13,12 +18,147 @@
     return jnp.dot(a, b, preferred_element_type=F32, precision=precision)
 
 
-def gather_blocks(block):
-    return lax.all_gather(block, "shard", axis=0, tiled=False)
-
-
-def sum_segments(value):
-    return lax.psum(value, "segment")
+MESH = pl.DeviceIdType.MESH
+
+
+def gather_kernel(side, count, *refs):
+    ins, outs = refs[:count], refs[count : 2 * count]
+    own_sem, near_send, near_recv, far_send, far_recv, core_send, core_recv = refs[2 * count :]
+    segment = lax.axis_index("segment")
+    me = lax.axis_index("shard")
+    core = lax.rem(me, 2)
+    y = lax.rem(me // 2, side)
+    z = me // (2 * side)
+
+    def device(zz, yy, cc):
+        return (segment, (zz * side + yy) * 2 + cc)
+
+    def turned(value, by):
+        return lax.rem(value + by + side, side)
+
+    y_peers = [None] + [device(z, turned(y, k), core) for k in range(1, side)]
+    z_peers = [None] + [device(turned(z, k), y, core) for k in range(1, side)]
+    partner = device(z, y, 1 - core)
+
+    barrier = pltpu.get_barrier_semaphore()
+    for peer in y_peers[1:] + z_peers[1:] + [partner]:
+        pl.semaphore_signal(barrier, inc=1, device_id=peer, device_id_type=MESH)
+    pl.semaphore_wait(barrier, 2 * side - 1)
+
+    def slab(i, k):
+        if i == 0:
+            return outs[i].at[turned(z, -k), :, core]
+        return outs[i].at[:, turned(y, -k), core]
+
+    def send(src, dst, send_sem, recv_sem, peer):
+        copy = pltpu.make_async_remote_copy(
+            src_ref=src,
+            dst_ref=dst,
+            send_sem=send_sem,
+            recv_sem=recv_sem,
+            device_id=peer,
+            device_id_type=MESH,
+        )
+        copy.start()
+        return copy
+
+    near, far, across, own = {}, {}, {}, {}
+    for k in range(1, side):
+        for i in range(count):
+            peers = y_peers if i == 0 else z_peers
+            near[i, k] = send(
+                ins[i], outs[i].at[z, y, core], near_send.at[i, k], near_recv.at[i, k], peers[k]
+            )
+    for i in range(count):
+        own[i] = pltpu.make_async_copy(ins[i], outs[i].at[z, y, core], own_sem.at[i])
+        own[i].start()
+    for i in range(count):
+        own[i].wait()
+        for k in range(1, side):
+            near[i, k].wait()
+        peers = z_peers if i == 0 else y_peers
+        for k in range(1, side):
+            far[i, k] = send(
+                slab(i, 0), slab(i, 0), far_send.at[i, k], far_recv.at[i, k], peers[k]
+            )
+        across[i, 0] = send(
+            slab(i, 0), slab(i, 0), core_send.at[i, 0], core_recv.at[i, 0], partner
+        )
+    for k in range(1, side):
+        for i in range(count):
+            far[i, k].wait()
+            across[i, k] = send(
+                slab(i, k), slab(i, k), core_send.at[i, k], core_recv.at[i, k], partner
+            )
+    for k in range(side):
+        for i in range(count):
+            across[i, k].wait()
+
+
+def gather_blocks(first, second, collective_id):
+    shard_count = lax.axis_size("shard")
+    side = math.isqrt(shard_count // 2)
+    sems = pltpu.SemaphoreType.DMA((2, side))
+    outs = pl.pallas_call(
+        functools.partial(gather_kernel, side, 2),
+        out_shape=[
+            jax.ShapeDtypeStruct((side, side, 2) + b.shape, b.dtype) for b in (first, second)
+        ],
+        in_specs=[pl.BlockSpec(memory_space=pltpu.VMEM)] * 2,
+        out_specs=[pl.BlockSpec(memory_space=pltpu.VMEM)] * 2,
+        scratch_shapes=[pltpu.SemaphoreType.DMA((2,))] + [sems] * 6,
+        compiler_params=pltpu.CompilerParams(collective_id=collective_id, has_side_effects=True),
+    )(first, second)
+    return [o.reshape((shard_count,) + o.shape[3:]) for o in outs]
+
+
+def sum_kernel(count, x_ref, out_ref, slots, own_sem, send_sem, recv_sem):
+    segment = lax.axis_index("segment")
+    me = lax.axis_index("shard")
+    peers = [(lax.rem(segment + k, count), me) for k in range(1, count)]
+    barrier = pltpu.get_barrier_semaphore()
+    for peer in peers:
+        pl.semaphore_signal(barrier, inc=1, device_id=peer, device_id_type=MESH)
+    pl.semaphore_wait(barrier, count - 1)
+    copies = []
+    for k, peer in enumerate(peers):
+        copies.append(
+            pltpu.make_async_remote_copy(
+                src_ref=x_ref,
+                dst_ref=slots.at[segment],
+                send_sem=send_sem.at[k],
+                recv_sem=recv_sem.at[k],
+                device_id=peer,
+                device_id_type=MESH,
+            )
+        )
+        copies[-1].start()
+    own = pltpu.make_async_copy(x_ref, slots.at[segment], own_sem)
+    own.start()
+    own.wait()
+    for copy in copies:
+        copy.wait()
+    total = slots[0]
+    for k in range(1, count):
+        total = total + slots[k]
+    out_ref[...] = total
+
+
+def sum_segments(value, collective_id):
+    count = lax.axis_size("segment")
+    return pl.pallas_call(
+        functools.partial(sum_kernel, count),
+        out_shape=jax.ShapeDtypeStruct(value.shape, value.dtype),
+        in_specs=[pl.BlockSpec(memory_space=pltpu.VMEM)],
+        out_specs=pl.BlockSpec(memory_space=pltpu.VMEM),
+        scratch_shapes=[
+            pltpu.VMEM((count,) + value.shape, value.dtype),
+            pltpu.SemaphoreType.DMA,
+            pltpu.SemaphoreType.DMA((count - 1,)),
+            pltpu.SemaphoreType.DMA((count - 1,)),
+        ],
+        compiler_params=pltpu.CompilerParams(collective_id=collective_id, has_side_effects=True),
+    )(value)
 
 
 def local(
@@ -61,20 +201,22 @@
     def part_of(values):
         return [fdot(values[:, g * span : (g + 1) * span], pick) for g in range(spans)]
 
-    def part_of32(values):
-        return jnp.concatenate(
-            [fdot(values[:, g * span : (g + 1) * span], pick32, HIGH) for g in range(spans)], 1
-        )
-
-    own_gain = jnp.concatenate(part_of(holder_attribute_factor), 0).astype(BF16)
+    wide = jnp.concatenate(
+        [holder_attribute_factor.astype(F32), block_result_offsets, block_grading_vectors], 0
+    )
+    wide = fdot(wide.reshape(7 * spans, span), pick32, HIGH)
+    own_gain = wide[:spans].astype(BF16)
+    wide = wide[spans:].reshape(6, part_width)
+    biases, heads = wide[:3], wide[3:]
     own_lower = lax.dynamic_slice_in_dim(block_lowering_matrices, segment_id * piece, piece, 1)
     own_raise = lax.dynamic_slice_in_dim(block_raising_flipped, segment_id * piece, piece, 1)
-    block = jnp.concatenate(
-        [own_lower.reshape(3 * piece, low_rank), own_raise.reshape(3 * piece, low_rank), own_gain], 0
-    )
-    blocks = gather_blocks(block)
-
-    def matrix(k):
+    lower_blocks, raise_blocks = gather_blocks(
+        own_lower.reshape(3 * piece, low_rank),
+        jnp.concatenate([own_raise.reshape(3 * piece, low_rank), own_gain], 0),
+        0,
+    )
+
+    def matrix(blocks, k):
         return blocks[:, k * piece : (k + 1) * piece].reshape(part_width, low_rank)
 
     hidden = jax.nn.relu(
@@ -93,9 +235,11 @@
     order = jnp.arange(entries, dtype=jnp.int32)
     same = (owner[:, :, None] == owner[:, None, :]) & (order[None, :] < order[:, None])
     within = jnp.sum(same.astype(jnp.int32), axis=2)
-    target = owner * cap_slots + within
-    slots = jnp.arange(shard_count * cap_slots, dtype=jnp.int32)
-    placed = slots[None, :, None] == target[:, None, :]
+    owners = jnp.arange(shard_count, dtype=jnp.int32)
+    places = jnp.arange(cap_slots, dtype=jnp.int32)
+    placed = (owner[:, None, None, :] == owners[:, None]) & (
+        within[:, None, None, :] == places[:, None, None]
+    )
 
     gate_col = gate.reshape(rows, 1)
     keep_col = keep.reshape(rows, 1)
@@ -105,13 +249,12 @@
         owner.reshape(rows, 1) == jnp.arange(shard_count, dtype=jnp.int32)[None, :]
     ).astype(BF16)
     gains = jnp.concatenate(
-        [fdot(owner_hot, blocks[:, 6 * piece + g]) for g in range(part_width // LANES)], 1
+        [fdot(owner_hot, raise_blocks[:, 3 * piece + g]) for g in range(part_width // LANES)], 1
     )
     x = (h0.astype(F32) * gains).astype(BF16)
 
-    biases = part_of32(block_result_offsets)
-    heads = part_of32(block_grading_vectors)
-    lower1, lower2, lower3, raise1, raise2, raise3 = [matrix(k) for k in range(6)]
+    lower1, lower2, lower3 = [matrix(lower_blocks, k) for k in range(3)]
+    raise1, raise2, raise3 = [matrix(raise_blocks, k) for k in range(3)]
 
     between = lax.dot_general(
         raise2, lower3, (((0,), (0,)), ((), ())), preferred_element_type=F32
@@ -136,7 +279,7 @@
     first = jnp.concatenate(
         [fdot(x, lower1), between, raised, raised3, lowered_bias, consts], 0
     )
-    first = sum_segments(jnp.pad(first, ((0, 3), (0, 0))))
+    first = sum_segments(jnp.pad(first, ((0, 3), (0, 0))), 1)
 
     act1 = first[:rows].astype(BF16)
     lifted = (
@@ -155,7 +298,7 @@
         ]
     ).reshape(-1, low_rank)
     second = jnp.concatenate([fdot(h1, lower2), fdot(h1, lower3), graded], 0)
-    second = sum_segments(jnp.pad(second, ((0, -second.shape[0] % 8), (0, 0))))
+    second = sum_segments(jnp.pad(second, ((0, -second.shape[0] % 8), (0, 0))), 2)
 
     between = first[rows : rows + low_rank]
     vectors = first[rows + low_rank : rows + low_rank + 5]
@@ -172,14 +315,13 @@
     )
     section = jnp.stack([gate.reshape(rows), graded[0], graded2 * keep_row, graded3 * keep_row])
     values = lax.dynamic_index_in_dim(section, segment_id, 0, keepdims=False)
-    values = values.reshape(rounds, 1, entries)
-    sent = jnp.sum(jnp.where(placed, values, 0.0), axis=2)
-    outgoing = sent.reshape(rounds, shard_count, cap_slots).transpose(1, 0, 2)
-    outgoing = outgoing.reshape(shard_count, rounds * cap_slots)
-    arrived = lax.all_to_all(outgoing, "shard", split_axis=0, concat_axis=0, tiled=True)
-    arrived = arrived.reshape(shard_count, rounds, cap_slots).transpose(1, 0, 2)
-    arrived = arrived.reshape(rounds, shard_count * cap_slots)
-    return jnp.where(segment_id == 0, sent, arrived)[None]
+    values = values.reshape(rounds, 1, 1, entries)
+    sent = jnp.sum(jnp.where(placed, values, 0.0), axis=3)
+    boards = jnp.stack(gather_blocks(sent[0], sent[1], 3))
+    mine = owners == lax.axis_index("shard")
+    arrived = jnp.sum(jnp.where(mine, boards, 0.0), axis=3)
+    result = jnp.where(segment_id == 0, sent.transpose(0, 2, 1), arrived)
+    return result.reshape(1, rounds, shard_count * cap_slots)
 
 
 def solution(mesh):

time: 262 us -> 143 us (0.55)
  waiting for transfers between devices: 164 us -> 0 us
  Pallas kernels: 0 us -> 87.9 us
  matrix products: 45.1 us -> 25.2 us
  starting transfers between devices: 16.4 us -> 0 us
  between operations: 13.4 us -> 0.41 us
  other arithmetic: 9.7 us -> 13.7 us
    psum x2 -> x0, waiting for transfers between devices: 97.2 us -> none  [sum_segments(): return lax.psum(value, 'segment')]
    pallas_call x0 -> x4, Pallas kernels: none -> 87.9 us  [the longest x2 55.1 us: gather_blocks(): pl.pallas_call(functools.partial(gather_kernel, side, 2), out_shape=[jax....]
    all_gather x1 -> x0, waiting for transfers between devices: 55.1 us -> none  [gather_blocks(): return lax.all_gather(block, 'shard', axis=0, tiled=False)]
    dot_general x45 -> x22, matrix products: 42.6 us -> 19.9 us  [fdot(): return jnp.dot(a, b, preferred_element_type=F32, precision=precision)]
    all_to_all x1 -> x0, starting transfers between devices: 16.3 us -> none  [local(): lax.all_to_all(outgoing, 'shard', split_axis=0, concat_axis=0, tiled=True)]
    all_to_all x1 -> x0, waiting for transfers between devices: 11.4 us -> none  [local(): lax.all_to_all(outgoing, 'shard', split_axis=0, concat_axis=0, tiled=True)]
    concatenate x1, local copies, waits for them, and re-layouts: 0.04 us -> 3.39 us  [local(): jnp.concatenate([fdot(x, lower1), between, raised, raised3, lowered_bias,...]
  transfers between devices with their start and end apart: 4 -> 0, of which waited for: 4 -> 0; matrix products, arithmetic and copies ran while one was open for 14% -> 0% of each run, Pallas kernels for 0% -> 0%
where the time goes in v2:
time: 143 us; the launch traced here: 142 us
  Pallas kernels  87.9 us (61%)
  matrix products  25.2 us (18%)
  local copies, waits for them, and re-layouts  14.9 us (10%)
  other arithmetic  13.7 us (10%)
    pallas_call x2, Pallas kernels, gather_blocks(): pl.pallas_call(functools.partial(gather_kernel, side, 2), out_shape=[jax....  55.1 us
    pallas_call x2, Pallas kernels, sum_segments(): pl.pallas_call(functools.partial(sum_kernel, count), out_shape=jax.ShapeD...  32.8 us
    dot_general x22, matrix products, fdot(): return jnp.dot(a, b, preferred_element_type=F32, precision=precision)  19.9 us
    concatenate x1, local copies, waits for them, and re-layouts, local(): jnp.concatenate([fdot(x, lower1), between, raised, raised3, lowered_bias,...  3.39 us
    slice x1, local copies, waits for them, and re-layouts, local(): raise_blocks[:, 3 * piece + g]  3.09 us

profile of v2, /device:TPU:1, one launch (start us, length us, event | category | flops | bytes accessed | tf_op | source)
XLA Modules:
  0.0 142.1 jit_solution(15843582693006327324)
XLA Ops:
  0.1 0.9 convert_element_type.60
  0.9 0.9 pad_maximum_fusion
  1.9 0.6 fusion.85
  2.6 1.3 dynamic-slice_bitcast_fusion
  3.9 0.6 pad_maximum_fusion.1.refs_1_
  4.5 37.5 %shard_map.127 = (bf16[8,8,2,24,128]{4,3,2,1,0:T(8,128)(2,1)}, bf16[8,8,2,32,128]{4,3,2,1,0:T(8,128)(2,1)}) custom-call(bf16[24,128]{1,0:T(8,128)(2,1)} %get-tuple-element.68.refs_0_, bf16[32,128]{1,0:T(8,128)(2,1)} %pad_maximum_fusion.1.refs_1_), custom_call_target="tpu_custom_call" | custom-call | tf_op jit(solution)/shard_map/pallas_call | solution.py:102
  42.0 3.1 %fusion.88 = (bf16[128,1,128]{2,1,0:T(2,128)(2,1)S(1)}, bf16[128,1,128]{2,1,0:T(2,128)(2,1)S(1)}, bf16[128,1,128]{2,1,0:T(2,128)(2,1)S(1)}, bf16[128,1,128]{2,1,...) fusion(bf16[128,32,128]{2,1,0:T(8,128)(2,1)} %bitcast.162), kind=kLoop, calls=%fused_computation.178 | loop fusion | bytes 524288 | tf_op jit(solution)/shard_map/slice | solution.py:252
  45.4 0.3 convolution_dynamic-update-slice_fusion.6
  45.6 0.3 convolution_dynamic-update-slice_fusion.5
  45.9 0.3 convolution_dynamic-update-slice_fusion.4
  46.1 0.3 convolution_dynamic-update-slice_fusion.3
  47.2 1.3 fusion.13
  48.5 1.3 fusion.12
  49.8 1.3 fusion.11
  51.1 1.3 fusion.10
  52.5 1.3 fusion.9
  53.8 1.3 fusion.8
  55.1 1.3 fusion.7
  56.4 1.3 fusion.6
  57.7 0.6 convert_bitcast_fusion
  58.4 4.4 %fusion = f32[1,1024]{1,0:T(1,128)S(1)} fusion(bf16[1024,1]{0,1:T(2,128)(2,1)S(1)} %reshape.213, f32[1024]{0:T(1024)S(1)} %copy-done.14, bf16[1024,1024]{1,0:T(8,128)(2,1)S(1)} %bitcast.156, bf16[1024,1024]{1,0:T(8,128)(2,1)} %param.19), kind=kOutput, calls=%fused_computation.1 | convolution fusion | flops 2152726528 | bytes 4204544 | tf_op jit(solution)/shard_map/dot_general | solution.py:18
  63.0 1.8 %multiply_convert_fusion = bf16[256,1024]{0,1:T(8,128)(2,1)S(1)} fusion(f32[256,1024]{0,1:T(8,128)} %copy-done.3, f32[256,1024]{0,1:T(8,128)} %fusion.6, f32[256]{0:T(256)S(1)} %bitcast.181), kind=kLoop, calls=%fused_computation.46 | loop fusion | flops 1310720 | bytes 2622464 | tf_op jit(solution)/shard_map/convert_element_type | solution.py:254
  64.9 0.3 fusion.33
  65.3 0.9 convolution_bitcast_fusion.8
  66.2 1.3 slice_bitcast_fusion.8
  67.5 0.8 fusion.32
  68.2 0.8 fusion.47
  69.0 0.6 slice.207
  69.6 1.2 fusion.49
  70.8 2.0 %fusion.73 = f32[1,128]{1,0:T(1,128)S(1)} fusion(f32[1]{0:T(128)} %bitcast.41, f32[1]{0:T(128)} %bitcast.40, f32[1]{0:T(128)} %bitcast.39), kind=kLoop, calls=%fused_computation.160 | loop fusion | flops 768 | bytes 524 | tf_op jit(solution)/shard_map/broadcast_in_dim | solution.py:278
  72.8 3.4 %concatenate.22 = f32[389,128]{1,0:T(8,128)} concatenate(f32[256,128]{1,0:T(8,128)S(1)} %fusion.33, f32[128,128]{1,0:T(8,128)} %convolution_bitcast_fusion.8, f32[2,128]{1,0:T(2,128)S(1)} %fusion.49, f32[1,128]{1,0:T(1,128)} %fusion.32, f32[1,128]{1,0:T(1,128)} %fusion.47, f32[1,128]{1,0:T(1,128)S(1)} %fusion.73), dimensions={0} | concatenate | bytes 398336 | tf_op jit(solution)/shard_map/concatenate | solution.py:279
  76.2 1.6 %pad.13.x_ref = f32[392,128]{1,0:T(8,128)} pad(f32[389,128]{1,0:T(8,128)} %concatenate.22, f32[]{:T(128)} %constant.73.clone.1), padding=0_3x0_0 | pad | bytes 399876 | tf_op jit(solution)/shard_map/jit(_pad)/pad | solution.py:282
  77.8 15.3 %shard_map.128 = f32[392,128]{1,0:T(8,128)} custom-call(f32[392,128]{1,0:T(8,128)} %pad.13.x_ref), custom_call_target="tpu_custom_call" | custom-call | tf_op jit(solution)/shard_map/pallas_call | solution.py:149
  93.1 1.7 %fusion.21 = (f32[256]{0:T(256)S(1)}, f32[256]{0:T(256)S(1)}, bf16[256,1024]{0,1:T(8,128)(2,1)S(1)}, f32[256]{0:T(256)S(1)}) fusion(f32[1024]{0:T(1024)} %get-tuple-element.43, f32[1024]{0:T(1024)} %get-tuple-element.45, f32[1024]{0:T(1024)} %get-tuple-element.42, f32[256]{0:T(256)} %get-tuple-element.21, f32[1024]{0:T(1024)} %get-tuple-element.44, ...), kind=kOutput, calls=%fused_computation.43 | convolution fusion | flops 70515968 | bytes 1396736 | tf_op jit(solution)/shard_map/dot_general | solution.py:286
  94.8 0.3 fusion.31
  95.2 0.3 fusion.45
  95.5 0.7 select_maximum_fusion.x_ref
  96.3 17.5 %shard_map.129 = f32[520,128]{1,0:T(8,128)} custom-call(f32[520,128]{1,0:T(8,128)} %select_maximum_fusion.x_ref), custom_call_target="tpu_custom_call" | custom-call | tf_op jit(solution)/shard_map/pallas_call | solution.py:149
  113.7 0.8 slice_bitcast_fusion.15
  114.6 1.3 fusion.20
  115.9 1.1 fusion.52
  117.0 0.8 fusion.89
  117.7 1.5 %fusion.90 = (f32[1,1]{1,0:T(1,128)}, f32[1,1]{1,0:T(1,128)}, f32[1,1]{1,0:T(1,128)}) fusion(f32[392,128]{1,0:T(8,128)} %shard_map.128), kind=kLoop, calls=%fused_computation.180 | loop fusion | bytes 24 | tf_op jit(solution)/shard_map/slice | solution.py:308
  119.2 1.9 %add_multiply_fusion.1 = (f32[1,256]{1,0:T(1,128)S(1)}, f32[1,256]{1,0:T(1,128)S(1)}) fusion(f32[1,256]{1,0:T(1,128)S(1)} %bitcast.194, f32[1,256]{1,0:T(1,128)S(1)} %bitcast.187, f32[1,256]{1,0:T(1,128)S(1)} %bitcast.183, f32[]{:T(128)} %bitcast.56, f32[]{:T(128)} %bitcast.65, f32[1,256]{1,0:T(1,128)S(1)} %bitcast.190, f32[]{:T(128)} %bitcast.61, ...), kind=kLoop, calls=%fused_computation.154 | loop fusion | flops 2304 | bytes 8204 | tf_op jit(solution)/shard_map/mul | solution.py:316
  121.6 0.6 slice_bitcast_fusion.11
  122.1 17.6 %shard_map.130 = (f32[8,8,2,2,128]{4,3,2,1,0:T(2,128)}, f32[8,8,2,2,128]{4,3,2,1,0:T(2,128)}) custom-call(f32[2,128]{1,0:T(2,128)} %get-tuple-element.52.refs_0_, f32[2,128]{1,0:T(2,128)} %get-tuple-element.51.refs_1_), custom_call_target="tpu_custom_call" | custom-call | tf_op jit(solution)/shard_map/pallas_call | solution.py:102
  139.8 1.3 fusion.42
  141.4 0.7 reshape.212
  (63 shorter events, 2.2 us)
Async XLA Ops:
  0.0 58.4 %copy-start = (bf16[2,512,1024]{2,1,0:T(8,128)(2,1)S(1)}, bf16[2,512,1024]{2,1,0:T(8,128)(2,1)}, u32[]{:S(2)}) copy-start(bf16[2,512,1024]{2,1,0:T(8,128)(2,1)} %param.13) | copy-start | bytes 6291460
  0.0 45.1 %copy-start.4 = (s32[2,128,1]{1,2,0:T(1,128)S(1)}, s32[2,128,1]{1,2,0:T(1,128)}, u32[]{:S(2)}) copy-start(s32[2,128,1]{1,2,0:T(1,128)} %param.17) | copy-start | bytes 3076
  2.6 47.3 %copy-start.5 = (f32[56,128]{1,0:T(8,128)}, f32[56,128]{1,0:T(8,128)S(1)}, u32[]{:S(2)}) copy-start(f32[56,128]{1,0:T(8,128)S(1)} %fusion.85) | copy-start | bytes 86020
  42.0 5.2 %copy-start.13 = (bf16[2,128,4096]{2,1,0:T(8,128)(2,1)S(1)}, bf16[2,128,4096]{2,1,0:T(8,128)(2,1)}, u32[]{:S(2)}) copy-start(bf16[2,128,4096]{2,1,0:T(8,128)(2,1)} %param.14) | copy-start | bytes 6291460
  47.2 5.3 %copy-start.3 = (f32[256,1024]{0,1:T(8,128)}, f32[256,1024]{0,1:T(8,128)S(1)}, u32[]{:S(2)}) copy-start(f32[256,1024]{0,1:T(8,128)S(1)} %convolution_dynamic-update-slice_fusion) | copy-start | bytes 3145732
  53.8 3.9 %copy-start.7 = (s32[2,128]{1,0:T(2,128)S(1)}, s32[2,128]{1,0:T(2,128)}, u32[]{:S(2)}) copy-start(s32[2,128]{1,0:T(2,128)} %param.15) | copy-start | bytes 3076
  53.8 3.9 %copy-start.12 = (s32[2,1]{0,1:T(1,128)S(1)}, s32[2,1]{0,1:T(1,128)}, u32[]{:S(2)}) copy-start(s32[2,1]{0,1:T(1,128)} %param.16) | copy-start | bytes 28
  53.8 4.6 %copy-start.8 = (bf16[1024]{0:T(1024)(128)(2,1)S(1)}, bf16[1024]{0:T(1024)(128)(2,1)}, u32[]{:S(2)}) copy-start(bf16[1024]{0:T(1024)(128)(2,1)} %param.21) | copy-start | bytes 6148
  53.8 4.6 %copy-start.14 = (f32[1024]{0:T(1024)S(1)}, f32[1024]{0:T(1024)}, u32[]{:S(2)}) copy-start(f32[1024]{0:T(1024)} %param.20) | copy-start | bytes 12292
  58.3 4.6 %copy-start.9 = (pred[2,128]{1,0:T(4,128)(4,1)}, pred[2,128]{1,0:T(4,128)(4,1)S(1)}, u32[]{:S(2)}) copy-start(pred[2,128]{1,0:T(4,128)(4,1)S(1)} %get-tuple-element.22) | copy-start | bytes 772
  62.8 2.1 %copy-start.1 = (bf16[8,8,2,24,128]{4,3,2,1,0:T(8,128)(2,1)S(1)}, bf16[8,8,2,24,128]{4,3,2,1,0:T(8,128)(2,1)}, u32[]{:S(2)}) copy-start(bf16[8,8,2,24,128]{4,3,2,1,0:T(8,128)(2,1)} %get-tuple-element.10) | copy-start | bytes 2359300
  62.8 2.4 %copy-start.2 = (bf16[8,8,2,32,128]{4,3,2,1,0:T(8,128)(2,1)S(1)}, bf16[8,8,2,32,128]{4,3,2,1,0:T(8,128)(2,1)}, u32[]{:S(2)}) copy-start(bf16[8,8,2,32,128]{4,3,2,1,0:T(8,128)(2,1)} %get-tuple-element.9) | copy-start | bytes 3145732
  63.0 3.2 %copy-start.6 = (f32[56,128]{1,0:T(8,128)S(1)}, f32[56,128]{1,0:T(8,128)}, u32[]{:S(2)}) copy-start(f32[56,128]{1,0:T(8,128)} %copy-done.5) | copy-start | bytes 86020
  64.8 4.2 %slice-start = ((f32[56,128]{1,0:T(8,128)}), f32[16,128]{1,0:T(8,128)S(1)}, s32[]{:S(2)}) async-start(f32[56,128]{1,0:T(8,128)} %copy-done.5), calls=%async_computation | async-start | bytes 16384 | tf_op jit(solution)/shard_map/slice | solution.py:263
  94.8 19.8 %copy-start.11 = (f32[256]{0:T(256)S(1)}, f32[256]{0:T(256)}, u32[]{:S(2)}) copy-start(f32[256]{0:T(256)} %get-tuple-element.21) | copy-start | bytes 3076
  94.8 24.4 %copy-start.10 = (pred[2,128]{1,0:T(4,128)(4,1)S(1)}, pred[2,128]{1,0:T(4,128)(4,1)}, u32[]{:S(2)}) copy-start(pred[2,128]{1,0:T(4,128)(4,1)} %copy-done.9) | copy-start | bytes 772

commit v3 on v2

v3 whole, which is shorter than its diff:
```python
import functools
import math

import jax
import jax.numpy as jnp
from jax import lax
from jax.experimental import pallas as pl
from jax.experimental.pallas import tpu as pltpu
from jax.sharding import PartitionSpec as P

F32 = jnp.float32
BF16 = jnp.bfloat16
HIGH = lax.Precision.HIGHEST
LANES = 128


def fdot(a, b, precision=None):
    return jnp.dot(a, b, preferred_element_type=F32, precision=precision)


MESH = pl.DeviceIdType.MESH


def gather_kernel(side, count, extra_in, extra_out, works, *refs):
    ins, given = refs[:count], refs[count : count + extra_in]
    refs = refs[count + extra_in :]
    outs, made = refs[:count], refs[count : count + extra_out]
    refs = refs[count + extra_out :]
    own_sem, near_send, near_recv, far_send, far_recv, core_send, core_recv = refs[:7]
    scratch = refs[7:]
    segment = lax.axis_index("segment")
    me = lax.axis_index("shard")
    core = lax.rem(me, 2)
    y = lax.rem(me // 2, side)
    z = me // (2 * side)

    def device(zz, yy, cc):
        return (segment, (zz * side + yy) * 2 + cc)

    def turned(value, by):
        return lax.rem(value + by + side, side)

    y_peers = [None] + [device(z, turned(y, k), core) for k in range(1, side)]
    z_peers = [None] + [device(turned(z, k), y, core) for k in range(1, side)]
    partner = device(z, y, 1 - core)

    barrier = pltpu.get_barrier_semaphore()
    for peer in y_peers[1:] + z_peers[1:] + [partner]:
        pl.semaphore_signal(barrier, inc=1, device_id=peer, device_id_type=MESH)
    pl.semaphore_wait(barrier, 2 * side - 1)

    def slab(i, k):
        if i == 0:
            return outs[i].at[turned(z, -k), :, core]
        return outs[i].at[:, turned(y, -k), core]

    def send(src, dst, send_sem, recv_sem, peer):
        copy = pltpu.make_async_remote_copy(
            src_ref=src,
            dst_ref=dst,
            send_sem=send_sem,
            recv_sem=recv_sem,
            device_id=peer,
            device_id_type=MESH,
        )
        copy.start()
        return copy

    near, far, across, own = {}, {}, {}, {}
    for k in range(1, side):
        for i in range(count):
            peers = y_peers if i == 0 else z_peers
            near[i, k] = send(
                ins[i], outs[i].at[z, y, core], near_send.at[i, k], near_recv.at[i, k], peers[k]
            )
    for i in range(count):
        own[i] = pltpu.make_async_copy(ins[i], outs[i].at[z, y, core], own_sem.at[i])
        own[i].start()
    if works:
        works[0](given, made, scratch)
    for i in range(count):
        own[i].wait()
        for k in range(1, side):
            near[i, k].wait()
        peers = z_peers if i == 0 else y_peers
        for k in range(1, side):
            far[i, k] = send(
                slab(i, 0), slab(i, 0), far_send.at[i, k], far_recv.at[i, k], peers[k]
            )
        across[i, 0] = send(
            slab(i, 0), slab(i, 0), core_send.at[i, 0], core_recv.at[i, 0], partner
        )
    if works:
        works[1](given, made, scratch)
    for k in range(1, side):
        for i in range(count):
            far[i, k].wait()
            across[i, k] = send(
                slab(i, k), slab(i, k), core_send.at[i, k], core_recv.at[i, k], partner
            )
    for k in range(side):
        for i in range(count):
            across[i, k].wait()


def gather_blocks(first, second, collective_id, given=(), made=(), scratch=(), works=None):
    shard_count = lax.axis_size("shard")
    side = math.isqrt(shard_count // 2)
    sems = pltpu.SemaphoreType.DMA((2, side))
    outs = pl.pallas_call(
        functools.partial(gather_kernel, side, 2, len(given), len(made), works),
        out_shape=[
            jax.ShapeDtypeStruct((side, side, 2) + b.shape, b.dtype) for b in (first, second)
        ]
        + list(made),
        in_specs=[pl.BlockSpec(memory_space=pltpu.VMEM)] * (2 + len(given)),
        out_specs=[pl.BlockSpec(memory_space=pltpu.VMEM)] * (2 + len(made)),
        scratch_shapes=[pltpu.SemaphoreType.DMA((2,))] + [sems] * 6 + list(scratch),
        compiler_params=pltpu.CompilerParams(
            collective_id=collective_id, has_side_effects=True, vmem_limit_bytes=48 * 2**20
        ),
    )(first, second, *given)
    return [o.reshape((shard_count,) + o.shape[3:]) for o in outs[:2]] + list(outs[2:])


def prerank_work(given, made, scratch):
    attributes, inner, offset, grading = given[:4]
    (scores,) = scratch

    def step(t, carry):
        block = attributes[pl.ds(pl.multiple_of(t * LANES, LANES), LANES), :]
        hidden = jnp.maximum(fdot(block, inner[...]) + offset[...], 0.0).astype(BF16)
        scores[t] = lax.dot_general(
            grading[...], hidden, (((1,), (1,)), ((), ())), preferred_element_type=F32
        )
        return carry

    lax.fori_loop(0, attributes.shape[0] // LANES, step, 0)


def gate_work(rounds, given, made, scratch):
    positions, keep, rows, pick = given[4:]
    gates, gated = made
    (scores,) = scratch
    entries = rows.shape[0] // rounds
    steps = scores.shape[0] // rounds
    span = pick.shape[0]
    for r in range(rounds):
        here = pl.ds(r * entries, entries)
        looked_up = jnp.zeros((entries, LANES), F32)
        for t in range(steps):
            ids = lax.broadcasted_iota(jnp.int32, (entries, LANES), 1) + t * LANES
            row = scores[r * steps + t][0:1, :]
            looked_up += jnp.where(positions[here, :] == ids, row, 0.0)
        score = jnp.sum(looked_up, axis=1, keepdims=True)
        small = jnp.exp(-jnp.abs(score))
        gate = keep[here, :] * jnp.where(score >= 0.0, 1.0, small) / (1.0 + small)
        gates[here, :] = gate
        for g in range(rows.shape[1] // span):
            part = fdot(rows[here, g * span : (g + 1) * span], pick[...])
            gated[here, g * LANES : (g + 1) * LANES] = (part * gate).astype(BF16)


NT = (((1,), (1,)), ((), ()))


def section_kernel(
    count,
    h0,
    keep,
    keep_row,
    owner,
    gain,
    wide,
    lower1,
    lower2,
    lower3,
    raise1,
    raise2,
    raise3,
    out_ref,
    x_ref,
    out1_ref,
    slots1,
    slots2,
    slots3,
    send_sem,
    recv_sem,
):
    segment = lax.axis_index("segment")
    me = lax.axis_index("shard")
    rows, width = x_ref.shape
    low_rank = lower1.shape[1]
    owners = gain.shape[0] * LANES // width
    per = width // LANES
    peers = [(lax.rem(segment + k, count), me) for k in range(1, count)]
    barrier = pltpu.get_barrier_semaphore()
    for peer in peers:
        pl.semaphore_signal(barrier, inc=1, device_id=peer, device_id_type=MESH)

    def exchange(number, slots):
        copies = []
        for k, peer in enumerate(peers):
            copies.append(
                pltpu.make_async_remote_copy(
                    src_ref=slots.at[segment],
                    dst_ref=slots.at[segment],
                    send_sem=send_sem.at[number, k],
                    recv_sem=recv_sem.at[number, k],
                    device_id=peer,
                    device_id_type=MESH,
                )
            )
            copies[-1].start()
        return copies

    def total(slots, start, size):
        value = slots[0, start : start + size]
        for k in range(1, count):
            value = value + slots[k, start : start + size]
        return value

    owner_hot = (
        owner[...] == lax.broadcasted_iota(jnp.int32, (rows, owners), 1)
    ).astype(F32).astype(BF16)
    for g in range(per):
        gain_g = gain[pl.ds(g, owners, stride=per), :].astype(BF16)
        lanes = slice(g * LANES, (g + 1) * LANES)
        x_ref[:, lanes] = (h0[:, lanes].astype(F32) * fdot(owner_hot, gain_g)).astype(BF16)
    slots1[segment] = fdot(x_ref[...], lower1[...])
    pl.semaphore_wait(barrier, count - 1)
    first = exchange(0, slots1)

    table = wide[...]
    slots2[segment, 0:low_rank] = lax.dot_general(
        raise2[...], lower3[...], (((0,), (0,)), ((), ())), preferred_element_type=F32
    )
    for n, matrix in enumerate((raise2, raise3, lower3)):
        at = low_rank + 8 * n
        slots2[segment, at : at + 8] = fdot(table, matrix[...].astype(F32), HIGH)
    consts = [
        jnp.sum(table[a : a + 1] * table[b : b + 1], axis=1, keepdims=True)
        for a, b in ((1, 4), (1, 5), (2, 5))
    ]
    row = lax.broadcasted_iota(jnp.int32, (8, low_rank), 0)
    slots2[segment, low_rank + 24 : low_rank + 32] = jnp.where(
        row == 0, consts[0], jnp.where(row == 1, consts[1], consts[2])
    )
    for copy in first:
        copy.wait()
    weights = exchange(1, slots2)

    act1 = total(slots1, 0, rows).astype(BF16)
    for g in range(per):
        lanes = slice(g * LANES, (g + 1) * LANES)
        lifted = (
            lax.dot_general(act1, raise1[lanes, :], NT, preferred_element_type=F32)
            + table[0:1, lanes]
        )
        x32 = x_ref[:, lanes].astype(F32)
        out1 = (x32 + x32 * lifted) * keep[...]
        out1_ref[:, lanes] = out1
        x_ref[:, lanes] = out1.astype(BF16)
    h1 = x_ref[...]
    slots3[segment, 0:rows] = fdot(h1, lower2[...])
    slots3[segment, rows : 2 * rows] = fdot(h1, lower3[...])
    graded1 = lax.dot_general(table, out1_ref[...], NT, precision=HIGH, preferred_element_type=F32)
    graded = lax.dot_general(
        table, h1.astype(F32), NT, precision=HIGH, preferred_element_type=F32
    )
    which = lax.broadcasted_iota(jnp.int32, graded.shape, 0)
    graded = jnp.where(which == 3, graded1, graded)
    for c in range(rows // LANES):
        at = 2 * rows + 8 * c
        slots3[segment, at : at + 8] = graded[:, c * LANES : (c + 1) * LANES]
    for copy in weights:
        copy.wait()
    between = total(slots2, 0, low_rank)
    raised2 = total(slots2, low_rank, 8)
    raised3 = total(slots2, low_rank + 8, 8)
    lowered = total(slots2, low_rank + 16, 8)
    consts = total(slots2, low_rank + 24, 8)
    for copy in exchange(2, slots3):
        copy.wait()

    act2 = jnp.maximum(total(slots3, 0, rows), 0.0).astype(BF16).astype(F32)
    inner3 = (
        total(slots3, rows, rows) + fdot(act2, between, HIGH) + lowered[1:2]
    ) * keep[...]
    act3 = jnp.maximum(inner3, 0.0).astype(BF16).astype(F32)
    from2 = lax.dot_general(raised2, act2, NT, precision=HIGH, preferred_element_type=F32)
    from3 = lax.dot_general(raised3, act3, NT, precision=HIGH, preferred_element_type=F32)
    for c in range(rows // LANES):
        lanes = slice(c * LANES, (c + 1) * LANES)
        graded = total(slots3, 2 * rows + 8 * c, 8)
        kept = keep_row[0:1, lanes]
        out_ref[0:1, lanes] = graded[3:4]
        out_ref[1:2, lanes] = (graded[4:5] + from2[4:5, lanes] + consts[0:1]) * kept
        out_ref[2:3, lanes] = (
            (graded[5:6] + from2[5:6, lanes] + consts[1:2]) * kept
            + from3[5:6, lanes]
            + consts[2:3]
        ) * kept


def run_sections(collective_id, *operands):
    count = lax.axis_size("segment")
    rows, width = operands[0].shape
    low_rank = operands[6].shape[1]
    sems = pltpu.SemaphoreType.DMA((3, count - 1))
    return pl.pallas_call(
        functools.partial(section_kernel, count),
        out_shape=jax.ShapeDtypeStruct((3, rows), F32),
        in_specs=[pl.BlockSpec(memory_space=pltpu.VMEM)] * len(operands),
        out_specs=pl.BlockSpec(memory_space=pltpu.VMEM),
        scratch_shapes=[
            pltpu.VMEM((rows, width), BF16),
            pltpu.VMEM((rows, width), F32),
            pltpu.VMEM((count, rows, low_rank), F32),
            pltpu.VMEM((count, low_rank + 32, low_rank), F32),
            pltpu.VMEM((count, 2 * rows + rows // LANES * 8, low_rank), F32),
            sems,
            sems,
        ],
        compiler_params=pltpu.CompilerParams(
            collective_id=collective_id, has_side_effects=True, vmem_limit_bytes=48 * 2**20
        ),
    )(*operands)


def local(
    proposal_attributes,
    keeper_ordering_vectors,
    keeper_positions,
    alive_tallies,
    holder_shards,
    holder_attribute_factor,
    early_inner_matrix,
    early_inner_offset,
    early_grading_vector,
    block_lowering_matrices,
    block_raising_flipped,
    block_result_offsets,
    block_grading_vectors,
):
    segment_id = lax.axis_index("segment")
    segment_count = lax.axis_size("segment")
    shard_count = lax.axis_size("shard")
    rounds, entries, width = keeper_ordering_vectors.shape
    candidates = proposal_attributes.shape[1]
    low_rank = block_lowering_matrices.shape[2]
    cap_slots = max(2, 2 * entries // shard_count)
    rows = rounds * entries
    own_features = width // shard_count
    piece = own_features // segment_count
    part_width = width // segment_count
    span = segment_count * LANES
    spans = width // span

    at = lax.broadcasted_iota(jnp.int32, (span, LANES), 0)
    to = lax.broadcasted_iota(jnp.int32, (span, LANES), 1)
    chosen = (at // own_features == to // piece) & (
        at % own_features == segment_id * piece + to % piece
    )
    pick = chosen.astype(BF16)
    pick32 = chosen.astype(F32)

    wide = jnp.concatenate(
        [holder_attribute_factor.astype(F32), block_result_offsets, block_grading_vectors], 0
    )
    wide = fdot(wide.reshape(7 * spans, span), pick32, HIGH)
    own_gain = wide[:spans].astype(BF16)
    wide = wide[spans:].reshape(6, part_width)
    own_lower = lax.dynamic_slice_in_dim(block_lowering_matrices, segment_id * piece, piece, 1)
    own_raise = lax.dynamic_slice_in_dim(block_raising_flipped, segment_id * piece, piece, 1)
    owner = holder_shards[:, :, 0]
    keep = (keeper_positions < alive_tallies).astype(F32)
    keep_col = keep.reshape(rows, 1)
    lower_blocks, raise_blocks, gate_col, h0 = gather_blocks(
        own_lower.reshape(3 * piece, low_rank),
        jnp.concatenate([own_raise.reshape(3 * piece, low_rank), own_gain], 0),
        0,
        (
            proposal_attributes.reshape(rounds * candidates, -1),
            early_inner_matrix,
            early_inner_offset[None],
            jnp.broadcast_to(early_grading_vector, (8,) + early_grading_vector.shape),
            keeper_positions.reshape(rows, 1),
            keep_col,
            keeper_ordering_vectors.reshape(rows, width),
            pick,
        ),
        (
            jax.ShapeDtypeStruct((rows, 1), F32),
            jax.ShapeDtypeStruct((rows, part_width), BF16),
        ),
        (pltpu.VMEM((rounds * candidates // LANES, 8, LANES), F32),),
        (prerank_work, functools.partial(gate_work, rounds)),
    )

    def matrix(blocks, k):
        return blocks[:, k * piece : (k + 1) * piece].reshape(part_width, low_rank)

    order = jnp.arange(entries, dtype=jnp.int32)
    same = (owner[:, :, None] == owner[:, None, :]) & (order[None, :] < order[:, None])
    within = jnp.sum(same.astype(jnp.int32), axis=2)
    owners = jnp.arange(shard_count, dtype=jnp.int32)
    places = jnp.arange(cap_slots, dtype=jnp.int32)
    placed = (owner[:, None, None, :] == owners[:, None]) & (
        within[:, None, None, :] == places[:, None, None]
    )

    gain = raise_blocks[:, 3 * piece :].astype(F32).reshape(-1, LANES)
    graded = run_sections(
        1,
        h0,
        keep_col,
        keep.reshape(1, rows),
        owner.reshape(rows, 1),
        gain,
        jnp.pad(wide, ((0, 2), (0, 0))),
        *[matrix(lower_blocks, k) for k in range(3)],
        *[matrix(raise_blocks, k) for k in range(3)],
    )
    section = jnp.concatenate([gate_col.reshape(1, rows), graded], 0)
    values = lax.dynamic_index_in_dim(section, segment_id, 0, keepdims=False)
    values = values.reshape(rounds, 1, 1, entries)
    sent = jnp.sum(jnp.where(placed, values, 0.0), axis=3)
    boards = jnp.stack(gather_blocks(sent[0], sent[1], 3))
    mine = owners == lax.axis_index("shard")
    arrived = jnp.sum(jnp.where(mine, boards, 0.0), axis=3)
    result = jnp.where(segment_id == 0, sent.transpose(0, 2, 1), arrived)
    return result.reshape(1, rounds, shard_count * cap_slots)


def solution(mesh):
    placed = (
        P(None, "shard", None),
        P(None, "shard", None),
        P(None, "shard"),
        P(None, "shard"),
        P(None, "shard", None),
        P("shard", None),
        P(),
        P(),
        P(),
        P(None, "shard", None),
        P(None, "shard", None),
        P(),
        P(),
    )
    return jax.shard_map(
        local, mesh=mesh, in_specs=placed, out_specs=P("segment", None, "shard"), check_vma=False
    )
```

time: 143 us -> 97.2 us (0.68)
  matrix products: 25.2 us -> 0.64 us
  other arithmetic: 13.7 us -> 4.09 us
  local copies, waits for them, and re-layouts: 14.9 us -> 6.26 us
  Pallas kernels: 87.9 us -> 85.6 us
    dot_general x22 -> x1, matrix products: 19.9 us -> 0.64 us  [fdot(): return jnp.dot(a, b, preferred_element_type=F32, precision=precision)]
    slice x8 -> x1, local copies, waits for them, and re-layouts: 6 us -> 0.01 us  [local(): wide = wide[spans:].reshape(6, part_width)]
    dot_general x5 -> x0, matrix products: 5.3 us -> none  [the longest x1 1.67 us: local(): lax.dot_general(act1, raise1, (((1,), (1,)), ((), ())), preferred_element...]
    mul x4 -> x0, other arithmetic: 3.81 us -> none  [the longest x1 1.9 us: local(): graded2 * keep_row]
    concatenate x1 -> x0, local copies, waits for them, and re-layouts: 3.39 us -> none  [local(): jnp.concatenate([fdot(x, lower1), between, raised, raised3, lowered_bias,...]
    unnamed x31 -> x6, local copies, waits for them, and re-layouts: 0.08 us -> 2.6 us
    pallas_call x4 -> x3, Pallas kernels: 87.9 us -> 85.6 us  [the longest x2 54.8 us: gather_blocks(): pl.pallas_call(functools.partial(gather_kernel, side, 2, len(given), len(...]
    broadcast_in_dim x1 -> x0, other arithmetic: 1.96 us -> none  [local(): consts = jnp.pad(consts, (0, low_rank - 3))[None]]
where the time goes in v3:
time: 97.2 us; the launch traced here: 96.8 us
  Pallas kernels  85.6 us (88%)
  local copies, waits for them, and re-layouts  6.26 us (6%)
  other arithmetic  4.09 us (4%)
    pallas_call x2, Pallas kernels, gather_blocks(): pl.pallas_call(functools.partial(gather_kernel, side, 2, len(given), len(...  54.8 us
    pallas_call x1, Pallas kernels, run_sections(): pl.pallas_call(functools.partial(section_kernel, count), out_shape=jax.Sh...  30.7 us
    unnamed x6, local copies, waits for them, and re-layouts  2.6 us

profile of v3, /device:TPU:1, one launch (start us, length us, event | category | flops | bytes accessed | tf_op | source)
XLA Modules:
  0.0 96.8 jit_solution(7881949745673727001)
XLA Ops:
  0.1 0.7 convert_element_type.18
  0.8 0.9 pad_maximum_fusion
  1.7 0.1 reshape.96
  1.8 0.6 fusion.11
  2.4 0.7 dynamic-slice_bitcast_fusion
  3.2 0.6 fusion.10.refs_9_
  3.8 0.8 compare_convert_fusion
  4.5 0.1 copy.26.refs_7_.keep
  4.7 0.8 copy.25.refs_6_
  5.5 0.7 broadcast_in_dim.33.refs_5_
  6.2 0.0 copy-start
  6.2 1.6 %copy-done = bf16[2,512,1024]{2,1,0:T(8,128)(2,1)S(1)} copy-done((bf16[2,512,1024]{2,1,0:T(8,128)(2,1)S(1)}, bf16[2,512,1024]{2,1,0:T(8,128)(2,1)}, u32[]{:S(2)}) %copy-start) | copy-done | bytes 2097176
  7.8 0.0 copy-start.1
  7.8 0.7 copy-done.1
  8.5 38.0 %shard_map.127 = (bf16[8,8,2,24,128]{4,3,2,1,0:T(8,128)(2,1)S(1)}, bf16[8,8,2,32,128]{4,3,2,1,0:T(8,128)(2,1)S(1)}, f32[256,1]{1,0:T(8,128)S(1)}, bf16[256,1024]{1,0:T(8,128)(2,1)S(1)}) custom-call(bf16[24,128]{1,0:T(8,128)(2,1)S(1)} %get-tuple-element.29.refs_0_, bf16[32,128]{1,0:T(8,128)(2,1)S(1)} %pad_maximum_fusion.1.refs_1_, ...), custom_call_target="tpu_custom_call" | custom-call | tf_op jit(solution)/shard_map/pallas_call | solution.py:110
  46.5 0.0 copy-start.2
  46.5 0.2 slice_bitcast_fusion
  46.6 0.1 slice_bitcast_fusion.3
  46.8 0.3 copy-done.2
  47.1 0.1 copy.28.owner
  47.3 30.7 %shard_map.128 = f32[3,256]{1,0:T(4,128)S(1)} custom-call(bf16[256,1024]{1,0:T(8,128)(2,1)S(1)} %get-tuple-element.12.h0, f32[256,1]{1,0:T(8,128)S(1)} %copy.26.refs_7_.keep, f32[1,256]{1,0:T(1,128)S(1)} %bitcast.49, s32[256,1]{1,0:T(8,128)S(1)} %copy.28.owner, f32[1024,128]{1,0:T(8,128)S(1)} %get-tuple-element.20.gain, f32[8,1024]{1,0:T(8,128)S(1)} %pad.4.wide, ...), custom_call_target="tpu_custom_call" | custom-call | tf_op jit(solution)/shard_map/pallas_call | solution.py:311
  78.0 0.1 reduce
  78.2 0.2 convert_reduce_fusion
  78.4 0.2 select_reduce_fusion
  78.6 16.9 %shard_map.129 = (f32[8,8,2,2,128]{4,3,2,1,0:T(2,128)S(1)}, f32[8,8,2,2,128]{4,3,2,1,0:T(2,128)S(1)}) custom-call(f32[2,128]{1,0:T(2,128)S(1)} %get-tuple-element.25.refs_0_, f32[2,128]{1,0:T(2,128)S(1)} %get-tuple-element.24.refs_1_), custom_call_target="tpu_custom_call" | custom-call | tf_op jit(solution)/shard_map/pallas_call | solution.py:110
  95.5 0.3 fusion.1
  95.8 0.1 copy.29
  95.9 0.1 copy.30
  96.1 0.7 reshape.114
  (18 shorter events, 0.1 us)
Async XLA Ops:
  6.2 1.6 %copy-start = (bf16[2,512,1024]{2,1,0:T(8,128)(2,1)S(1)}, bf16[2,512,1024]{2,1,0:T(8,128)(2,1)}, u32[]{:S(2)}) copy-start(bf16[2,512,1024]{2,1,0:T(8,128)(2,1)} %param.13) | copy-start | bytes 6291460
  7.8 0.7 copy-start.1
  46.5 0.7 copy-start.2

commit v4 on v3

--- a/solution.py
+++ b/solution.py
@@ -49,10 +49,10 @@
         pl.semaphore_signal(barrier, inc=1, device_id=peer, device_id_type=MESH)
     pl.semaphore_wait(barrier, 2 * side - 1)
 
-    def slab(i, k):
+    def slab(i, k, start=0, size=side):
         if i == 0:
-            return outs[i].at[turned(z, -k), :, core]
-        return outs[i].at[:, turned(y, -k), core]
+            return outs[i].at[turned(z, -k), pl.ds(start, size), core]
+        return outs[i].at[pl.ds(start, size), turned(y, -k), core]
 
     def send(src, dst, send_sem, recv_sem, peer):
         copy = pltpu.make_async_remote_copy(
@@ -66,6 +66,7 @@
         copy.start()
         return copy
 
+    relayed = side == 8
     near, far, across, own = {}, {}, {}, {}
     for k in range(1, side):
         for i in range(count):
@@ -84,6 +85,8 @@
             near[i, k].wait()
         peers = z_peers if i == 0 else y_peers
         for k in range(1, side):
+            if relayed and 2 < k < side - 2:
+                continue
             far[i, k] = send(
                 slab(i, 0), slab(i, 0), far_send.at[i, k], far_recv.at[i, k], peers[k]
             )
@@ -92,9 +95,30 @@
         )
     if works:
         works[1](given, made, scratch)
-    for k in range(1, side):
+    half = side // 2
+    order = [1, side - 1, 2, side - 2, 3, side - 3, half] if relayed else range(1, side)
+    for k in order:
         for i in range(count):
+            peers = z_peers if i == 0 else y_peers
             far[i, k].wait()
+            if relayed and k == half:
+                far[i, 0].wait()
+            if relayed and k in (2, side - 2):
+                to, number, start = (1, half, 0) if k == 2 else (side - 1, 0, half)
+                far[i, 3 if k == 2 else side - 3] = send(
+                    slab(i, k),
+                    slab(i, k),
+                    far_send.at[i, 3 if k == 2 else side - 3],
+                    far_recv.at[i, 3 if k == 2 else side - 3],
+                    peers[to],
+                )
+                far[i, number] = send(
+                    slab(i, k, start, half),
+                    slab(i, k, start, half),
+                    far_send.at[i, number],
+                    far_recv.at[i, number],
+                    peers[k],
+                )
             across[i, k] = send(
                 slab(i, k), slab(i, k), core_send.at[i, k], core_recv.at[i, k], partner
             )
@@ -183,7 +207,9 @@
     out1_ref,
     slots1,
     slots2,
+    part3,
     slots3,
+    slots4,
     send_sem,
     recv_sem,
 ):
@@ -262,8 +288,11 @@
         out1_ref[:, lanes] = out1
         x_ref[:, lanes] = out1.astype(BF16)
     h1 = x_ref[...]
-    slots3[segment, 0:rows] = fdot(h1, lower2[...])
-    slots3[segment, rows : 2 * rows] = fdot(h1, lower3[...])
+    quarter = rows // count
+    for n, matrix in enumerate((lower2, lower3)):
+        product = fdot(h1, matrix[...])
+        for k in range(count):
+            part3[k, n * quarter : (n + 1) * quarter] = product[k * quarter : (k + 1) * quarter]
     graded1 = lax.dot_general(table, out1_ref[...], NT, precision=HIGH, preferred_element_type=F32)
     graded = lax.dot_general(
         table, h1.astype(F32), NT, precision=HIGH, preferred_element_type=F32
@@ -271,8 +300,10 @@
     which = lax.broadcasted_iota(jnp.int32, graded.shape, 0)
     graded = jnp.where(which == 3, graded1, graded)
     for c in range(rows // LANES):
-        at = 2 * rows + 8 * c
-        slots3[segment, at : at + 8] = graded[:, c * LANES : (c + 1) * LANES]
+        at = 2 * quarter + 8 * c
+        for k in range(count):
+            part3[k, at : at + 8] = graded[:, c * LANES : (c + 1) * LANES]
+    slots3[segment] = part3[segment]
     for copy in weights:
         copy.wait()
     between = total(slots2, 0, low_rank)
@@ -280,34 +311,58 @@
     raised3 = total(slots2, low_rank + 8, 8)
     lowered = total(slots2, low_rank + 16, 8)
     consts = total(slots2, low_rank + 24, 8)
-    for copy in exchange(2, slots3):
+    copies = []
+    for k, peer in enumerate(peers):
+        copies.append(
+            pltpu.make_async_remote_copy(
+                src_ref=part3.at[peer[0]],
+                dst_ref=slots3.at[segment],
+                send_sem=send_sem.at[2, k],
+                recv_sem=recv_sem.at[2, k],
+                device_id=peer,
+                device_id_type=MESH,
+            )
+        )
+        copies[-1].start()
+    for copy in copies:
         copy.wait()
 
-    act2 = jnp.maximum(total(slots3, 0, rows), 0.0).astype(BF16).astype(F32)
+    begin = pl.multiple_of(segment * quarter, quarter)
+    act2 = jnp.maximum(total(slots3, 0, quarter), 0.0).astype(BF16).astype(F32)
     inner3 = (
-        total(slots3, rows, rows) + fdot(act2, between, HIGH) + lowered[1:2]
-    ) * keep[...]
+        total(slots3, quarter, quarter) + fdot(act2, between, HIGH) + lowered[1:2]
+    ) * keep[pl.ds(begin, quarter), :]
     act3 = jnp.maximum(inner3, 0.0).astype(BF16).astype(F32)
+    act2 = jnp.concatenate([act2] * count, 0)
+    act3 = jnp.concatenate([act3] * count, 0)
     from2 = lax.dot_general(raised2, act2, NT, precision=HIGH, preferred_element_type=F32)
     from3 = lax.dot_general(raised3, act3, NT, precision=HIGH, preferred_element_type=F32)
+    row = lax.broadcasted_iota(jnp.int32, (8, LANES), 0)
+    lane = lax.broadcasted_iota(jnp.int32, (8, LANES), 1)
     for c in range(rows // LANES):
         lanes = slice(c * LANES, (c + 1) * LANES)
-        graded = total(slots3, 2 * rows + 8 * c, 8)
+        graded = total(slots3, 2 * quarter + 8 * c, 8)
         kept = keep_row[0:1, lanes]
-        out_ref[0:1, lanes] = graded[3:4]
-        out_ref[1:2, lanes] = (graded[4:5] + from2[4:5, lanes] + consts[0:1]) * kept
-        out_ref[2:3, lanes] = (
+        second = (graded[4:5] + from2[4:5, lanes] + consts[0:1]) * kept
+        third = (
             (graded[5:6] + from2[5:6, lanes] + consts[1:2]) * kept
             + from3[5:6, lanes]
             + consts[2:3]
         ) * kept
+        value = jnp.where(row == 0, graded[3:4], jnp.where(row == 1, second, third))
+        mine = (lane + c * LANES >= begin) & (lane + c * LANES < begin + quarter)
+        slots4[segment, 8 * c : 8 * c + 8] = jnp.where(mine, value, 0.0)
+    for copy in exchange(3, slots4):
+        copy.wait()
+    for c in range(rows // LANES):
+        out_ref[:, c * LANES : (c + 1) * LANES] = total(slots4, 8 * c, 8)[0:3]
 
 
 def run_sections(collective_id, *operands):
     count = lax.axis_size("segment")
     rows, width = operands[0].shape
     low_rank = operands[6].shape[1]
-    sems = pltpu.SemaphoreType.DMA((3, count - 1))
+    sems = pltpu.SemaphoreType.DMA((4, count - 1))
     return pl.pallas_call(
         functools.partial(section_kernel, count),
         out_shape=jax.ShapeDtypeStruct((3, rows), F32),
@@ -318,7 +373,9 @@
             pltpu.VMEM((rows, width), F32),
             pltpu.VMEM((count, rows, low_rank), F32),
             pltpu.VMEM((count, low_rank + 32, low_rank), F32),
-            pltpu.VMEM((count, 2 * rows + rows // LANES * 8, low_rank), F32),
+            pltpu.VMEM((count, 2 * rows // count + rows // LANES * 8, low_rank), F32),
+            pltpu.VMEM((count, 2 * rows // count + rows // LANES * 8, low_rank), F32),
+            pltpu.VMEM((count, rows // LANES * 8, low_rank), F32),
             sems,
             sems,
         ],

time: 97.2 us -> 90.8 us (0.934)
  Pallas kernels: 85.6 us -> 79.1 us
    pallas_call x1, Pallas kernels: 30.7 us -> 23.7 us  [run_sections(): pl.pallas_call(functools.partial(section_kernel, count), out_shape=jax.Sh...]
where the time goes in v4:
time: 90.8 us; the launch traced here: 90.3 us
  Pallas kernels  79.1 us (87%)
  local copies, waits for them, and re-layouts  6.26 us (7%)
  other arithmetic  4.09 us (5%)
    pallas_call x2, Pallas kernels, gather_blocks(): pl.pallas_call(functools.partial(gather_kernel, side, 2, len(given), len(...  55.4 us
    pallas_call x1, Pallas kernels, run_sections(): pl.pallas_call(functools.partial(section_kernel, count), out_shape=jax.Sh...  23.7 us
    unnamed x6, local copies, waits for them, and re-layouts  2.6 us

profile of v4, /device:TPU:1, one launch (start us, length us, event | category | flops | bytes accessed | tf_op | source)
XLA Modules:
  0.0 90.3 jit_solution(1799930225616995369)
XLA Ops:
  0.1 0.7 convert_element_type.18
  0.8 0.9 %pad_maximum_fusion = f32[7,4096]{1,0:T(8,128)S(1)} fusion(f32[3,4096]{1,0:T(4,128)} %param.25, f32[3,4096]{1,0:T(4,128)} %param.24, f32[1,4096]{1,0:T(1,128)S(1)} %convert_element_type.18), kind=kLoop, calls=%fused_computation.14 | loop fusion | flops 57344 | bytes 229376 | tf_op jit(solution)/shard_map/concatenate | solution.py:425
  1.7 0.1 reshape.96
  1.8 0.6 fusion.11
  2.4 0.7 dynamic-slice_bitcast_fusion
  3.2 0.6 fusion.10.refs_9_
  3.8 0.8 compare_convert_fusion
  4.5 0.1 copy.26.refs_7_.keep
  4.7 0.8 copy.25.refs_6_
  5.5 0.7 broadcast_in_dim.33.refs_5_
  6.2 0.0 copy-start
  6.2 1.6 %copy-done = bf16[2,512,1024]{2,1,0:T(8,128)(2,1)S(1)} copy-done((bf16[2,512,1024]{2,1,0:T(8,128)(2,1)S(1)}, bf16[2,512,1024]{2,1,0:T(8,128)(2,1)}, u32[]{:S(2)}) %copy-start) | copy-done | bytes 2097176
  7.8 0.0 copy-start.1
  7.8 0.7 copy-done.1
  8.5 33.9 %shard_map.127 = (bf16[8,8,2,24,128]{4,3,2,1,0:T(8,128)(2,1)S(1)}, bf16[8,8,2,32,128]{4,3,2,1,0:T(8,128)(2,1)S(1)}, f32[256,1]{1,0:T(8,128)S(1)}, bf16[256,1024]{1,0:T(8,128)(2,1)S(1)}) custom-call(bf16[24,128]{1,0:T(8,128)(2,1)S(1)} %get-tuple-element.29.refs_0_, bf16[32,128]{1,0:T(8,128)(2,1)S(1)} %pad_maximum_fusion.1.refs_1_, ...), custom_call_target="tpu_custom_call" | custom-call | tf_op jit(solution)/shard_map/pallas_call | solution.py:134
  42.4 0.0 copy-start.2
  42.4 0.2 slice_bitcast_fusion
  42.6 0.1 slice_bitcast_fusion.3
  42.8 0.3 copy-done.2
  43.1 0.1 copy.28.owner
  43.2 23.7 %shard_map.128 = f32[3,256]{1,0:T(4,128)S(1)} custom-call(bf16[256,1024]{1,0:T(8,128)(2,1)S(1)} %get-tuple-element.12.h0, f32[256,1]{1,0:T(8,128)S(1)} %copy.26.refs_7_.keep, f32[1,256]{1,0:T(1,128)S(1)} %bitcast.49, s32[256,1]{1,0:T(8,128)S(1)} %copy.28.owner, f32[1024,128]{1,0:T(8,128)S(1)} %get-tuple-element.20.gain, f32[8,1024]{1,0:T(8,128)S(1)} %pad.4.wide, ...), custom_call_target="tpu_custom_call" | custom-call | tf_op jit(solution)/shard_map/pallas_call | solution.py:366
  66.9 0.1 reduce
  67.1 0.2 convert_reduce_fusion
  67.3 0.2 select_reduce_fusion
  67.5 21.5 %shard_map.129 = (f32[8,8,2,2,128]{4,3,2,1,0:T(2,128)S(1)}, f32[8,8,2,2,128]{4,3,2,1,0:T(2,128)S(1)}) custom-call(f32[2,128]{1,0:T(2,128)S(1)} %get-tuple-element.25.refs_0_, f32[2,128]{1,0:T(2,128)S(1)} %get-tuple-element.24.refs_1_), custom_call_target="tpu_custom_call" | custom-call | tf_op jit(solution)/shard_map/pallas_call | solution.py:134
  89.0 0.3 fusion.1
  89.4 0.1 copy.29
  89.4 0.1 copy.30
  89.6 0.7 reshape.114
  (18 shorter events, 0.1 us)
Async XLA Ops:
  6.2 1.6 %copy-start = (bf16[2,512,1024]{2,1,0:T(8,128)(2,1)S(1)}, bf16[2,512,1024]{2,1,0:T(8,128)(2,1)}, u32[]{:S(2)}) copy-start(bf16[2,512,1024]{2,1,0:T(8,128)(2,1)} %param.13) | copy-start | bytes 6291460
  7.8 0.7 copy-start.1
  42.4 0.7 copy-start.2

commit v5 on v4

--- a/solution.py
+++ b/solution.py
@@ -66,7 +66,7 @@
         copy.start()
         return copy
 
-    relayed = side == 8
+    relayed = side == 8 and bool(works)
     near, far, across, own = {}, {}, {}, {}
     for k in range(1, side):
         for i in range(count):

time: 90.8 us -> 88 us (0.969)
  Pallas kernels: 79.1 us -> 76.4 us
    pallas_call x2, Pallas kernels: 55.4 us -> 52.7 us  [gather_blocks(): pl.pallas_call(functools.partial(gather_kernel, side, 2, len(given), len(...]
where the time goes in v5:
time: 88 us; the launch traced here: 87.6 us
  Pallas kernels  76.4 us (87%)
  local copies, waits for them, and re-layouts  6.26 us (7%)
  other arithmetic  4.09 us (5%)
    pallas_call x2, Pallas kernels, gather_blocks(): pl.pallas_call(functools.partial(gather_kernel, side, 2, len(given), len(...  52.7 us
    pallas_call x1, Pallas kernels, run_sections(): pl.pallas_call(functools.partial(section_kernel, count), out_shape=jax.Sh...  23.7 us
    unnamed x6, local copies, waits for them, and re-layouts  2.6 us

profile of v5, /device:TPU:1, one launch (start us, length us, event | category | flops | bytes accessed | tf_op | source)
XLA Modules:
  0.0 87.6 jit_solution(4536035562252562759)
XLA Ops:
  0.1 0.7 convert_element_type.18
  0.8 0.9 %pad_maximum_fusion = f32[7,4096]{1,0:T(8,128)S(1)} fusion(f32[3,4096]{1,0:T(4,128)} %param.25, f32[3,4096]{1,0:T(4,128)} %param.24, f32[1,4096]{1,0:T(1,128)S(1)} %convert_element_type.18), kind=kLoop, calls=%fused_computation.14 | loop fusion | flops 57344 | bytes 229376 | tf_op jit(solution)/shard_map/concatenate | solution.py:425
  1.7 0.1 reshape.96
  1.8 0.6 fusion.11
  2.4 0.7 dynamic-slice_bitcast_fusion
  3.2 0.6 fusion.10.refs_9_
  3.8 0.8 compare_convert_fusion
  4.5 0.1 copy.26.refs_7_.keep
  4.7 0.8 copy.25.refs_6_
  5.5 0.7 broadcast_in_dim.33.refs_5_
  6.2 0.0 copy-start
  6.2 1.6 %copy-done = bf16[2,512,1024]{2,1,0:T(8,128)(2,1)S(1)} copy-done((bf16[2,512,1024]{2,1,0:T(8,128)(2,1)S(1)}, bf16[2,512,1024]{2,1,0:T(8,128)(2,1)}, u32[]{:S(2)}) %copy-start) | copy-done | bytes 2097176
  7.8 0.0 copy-start.1
  7.8 0.7 copy-done.1
  8.5 33.9 %shard_map.127 = (bf16[8,8,2,24,128]{4,3,2,1,0:T(8,128)(2,1)S(1)}, bf16[8,8,2,32,128]{4,3,2,1,0:T(8,128)(2,1)S(1)}, f32[256,1]{1,0:T(8,128)S(1)}, bf16[256,1024]{1,0:T(8,128)(2,1)S(1)}) custom-call(bf16[24,128]{1,0:T(8,128)(2,1)S(1)} %get-tuple-element.29.refs_0_, bf16[32,128]{1,0:T(8,128)(2,1)S(1)} %pad_maximum_fusion.1.refs_1_, ...), custom_call_target="tpu_custom_call" | custom-call | tf_op jit(solution)/shard_map/pallas_call | solution.py:134
  42.4 0.0 copy-start.2
  42.4 0.2 slice_bitcast_fusion
  42.6 0.1 slice_bitcast_fusion.3
  42.8 0.3 copy-done.2
  43.1 0.1 copy.28.owner
  43.2 23.7 %shard_map.128 = f32[3,256]{1,0:T(4,128)S(1)} custom-call(bf16[256,1024]{1,0:T(8,128)(2,1)S(1)} %get-tuple-element.12.h0, f32[256,1]{1,0:T(8,128)S(1)} %copy.26.refs_7_.keep, f32[1,256]{1,0:T(1,128)S(1)} %bitcast.49, s32[256,1]{1,0:T(8,128)S(1)} %copy.28.owner, f32[1024,128]{1,0:T(8,128)S(1)} %get-tuple-element.20.gain, f32[8,1024]{1,0:T(8,128)S(1)} %pad.4.wide, ...), custom_call_target="tpu_custom_call" | custom-call | tf_op jit(solution)/shard_map/pallas_call | solution.py:366
  66.9 0.1 reduce
  67.1 0.2 convert_reduce_fusion
  67.3 0.2 select_reduce_fusion
  67.5 18.8 %shard_map.129 = (f32[8,8,2,2,128]{4,3,2,1,0:T(2,128)S(1)}, f32[8,8,2,2,128]{4,3,2,1,0:T(2,128)S(1)}) custom-call(f32[2,128]{1,0:T(2,128)S(1)} %get-tuple-element.25.refs_0_, f32[2,128]{1,0:T(2,128)S(1)} %get-tuple-element.24.refs_1_), custom_call_target="tpu_custom_call" | custom-call | tf_op jit(solution)/shard_map/pallas_call | solution.py:134
  86.3 0.3 fusion.1
  86.6 0.1 copy.29
  86.7 0.1 copy.30
  86.9 0.7 reshape.114
  (18 shorter events, 0.1 us)
Async XLA Ops:
  6.2 1.6 %copy-start = (bf16[2,512,1024]{2,1,0:T(8,128)(2,1)S(1)}, bf16[2,512,1024]{2,1,0:T(8,128)(2,1)}, u32[]{:S(2)}) copy-start(bf16[2,512,1024]{2,1,0:T(8,128)(2,1)} %param.13) | copy-start | bytes 6291460
  7.8 0.7 copy-start.1
  42.4 0.7 copy-start.2
